TPU v7x, 32 devices: a whole 2x2x4 slice. The times are simulated.
32 devices in a mesh: cand: 2 (over core), mp: 8 (over z, y), dp: 2 (over x).
Axes of the slice: x: 2, y: 2, z: 4, core: 2. Of those that a mesh axis runs over, the one named last changes fastest.
Arguments:
- clean: bfloat16 [1536, 768], P('mp', 'dp'), may hold values from -3 to 3
- noise: bfloat16 [1536, 768], P('mp', 'dp'), may hold values from -6 to 6
- level_index: int32 [12], P('dp'), may hold values from 0 to 31
- snap_first: bfloat16 [16, 9, 1536, 1536], P('cand', None, 'mp'), may hold values from -0.0546875 to 0.0546875
- snap_second: bfloat16 [16, 9, 1536, 1536], P('cand', None, 'mp'), may hold values from -0.0546875 to 0.0546875
- blend: float32 [4, 8], P('cand'), may hold values from -1.4 to 1.4
- snap_index: int32 [4, 8], P('cand'), may hold values from 0 to 15
Outputs:
- losses: float32 [4], P('cand')
- denoised: bfloat16 [4, 1536, 768], P('cand', 'mp', 'dp')
All inputs are finite; a program needn't handle non-finite values.
Results may differ from a plain program's by a relative error of at most 0.00265.
The roundings to bfloat16 on the way count: a program that leaves them out, or rounds other values in their place, can miss the bound.
Values may be sent and summed in bfloat16 or wider, within the bound.
A program may use at most 384 MiB of HBM per device.

v0:
```python
import jax
import jax.numpy as jnp
from jax import lax
from jax.sharding import PartitionSpec as P

LEVELS = 32


SIGMA_DATA = 0.5


def from_partner(value, axis, apart):
    return lax.ppermute(value, axis, [(i, i ^ 1 << apart) for i in range(lax.axis_size(axis))])


def noise_scale(level_index):
    ratio = 2.0 * level_index.astype(jnp.float32) / (LEVELS - 1) - 1.0
    return jnp.exp(-0.4 + 2.0 * ratio)


def tap_shift(values, down_by, right_by):
    length_all = values.shape[-1]
    offset = down_by * 8 + right_by
    padded = jnp.pad(values, [(0, 0)] * (values.ndim - 1) + [(9, 9)])
    moved = lax.slice_in_dim(padded, 9 + offset, 9 + offset + length_all, axis=values.ndim - 1)
    within = jnp.arange(length_all) % 64
    map_row = within // 8
    map_col = within % 8
    inside = (
        (map_row + down_by >= 0)
        & (map_row + down_by < 8)
        & (map_col + right_by >= 0)
        & (map_col + right_by < 8)
    )
    return jnp.where(inside, moved, jnp.zeros_like(moved))


def tap_stack(values):
    return jnp.stack(
        [tap_shift(values, down_by, right_by) for down_by in (-1, 0, 1) for right_by in (-1, 0, 1)],
        0,
    )


def blend_owned(first_own, second_own, mixing, first_slot):
    members = mixing.shape[0]
    shape = (members,) + first_own.shape[1:]

    def accumulate(which, totals):
        coeff = lax.dynamic_slice_in_dim(mixing, first_slot + which, 1, 1)[:, 0][
            :, None, None, None
        ]
        first_snap = lax.dynamic_index_in_dim(first_own, which, 0, keepdims=False).astype(
            jnp.float32
        )
        second_snap = lax.dynamic_index_in_dim(second_own, which, 0, keepdims=False).astype(
            jnp.float32
        )
        return (totals[0] + coeff * first_snap[None], totals[1] + coeff * second_snap[None])

    empty = jnp.zeros(shape, jnp.float32)
    return lax.fori_loop(0, first_own.shape[0], accumulate, (empty, empty))


def on_device(clean, noise, level_index, snap_first, snap_second, blend, snap_index):
    sigmas = jnp.repeat(noise_scale(level_index), 64)
    spread = sigmas * sigmas + SIGMA_DATA * SIGMA_DATA
    scale_in = 1.0 / jnp.sqrt(spread)
    scale_skip = SIGMA_DATA * SIGMA_DATA / spread
    scale_out = sigmas * SIGMA_DATA / jnp.sqrt(spread)
    weighting = spread / (sigmas * SIGMA_DATA) ** 2
    clean_f = clean.astype(jnp.float32)
    noisy = clean_f + sigmas * noise.astype(jnp.float32)
    x_own = (scale_in * noisy).astype(jnp.bfloat16)
    x_full = lax.all_gather(x_own, "mp", axis=0, tiled=True)
    x_stack = tap_stack(x_full)
    owned = snap_first.shape[0]
    stored = owned * lax.axis_size("cand")
    onehot = (snap_index[:, :, None] == jnp.arange(stored, dtype=jnp.int32)[None, None, :]).astype(
        jnp.float32
    )
    mixing = jnp.sum(blend[:, :, None] * onehot, 1)
    first_slot = lax.axis_index("cand") * owned
    other_mix = from_partner(mixing, "cand", 0)
    mine_first, mine_second = blend_owned(snap_first, snap_second, mixing, first_slot)
    give_first, give_second = blend_owned(snap_first, snap_second, other_mix, first_slot)
    got_first, got_second = from_partner((give_first, give_second), "cand", 0)
    first_w = (mine_first + got_first).astype(jnp.bfloat16)
    second_w = (mine_second + got_second).astype(jnp.bfloat16)
    preact = jnp.einsum("gkoc,kct->got", first_w, x_stack, preferred_element_type=jnp.float32)
    hidden = jax.nn.silu(preact).astype(jnp.bfloat16)
    h_stack = tap_stack(hidden)
    members = blend.shape[0]

    def member_feature(member):
        w_part = second_w[member]
        return lax.psum_scatter(
            jnp.einsum(
                "kio,kit->ot", w_part, h_stack[:, member], preferred_element_type=jnp.float32
            ),
            "mp",
            scatter_dimension=0,
            tiled=True,
        )

    features = jnp.stack([member_feature(member) for member in range(members)], 0)
    denoised_f = scale_skip[None, None, :] * noisy[None] + scale_out[None, None, :] * features
    partial_value = jnp.sum(
        weighting[None, None, :] * (denoised_f - clean_f[None]) ** 2, axis=(1, 2)
    )
    entries = clean.shape[0] * lax.axis_size("mp") * clean.shape[1] * lax.axis_size("dp")
    totals = jnp.stack(
        [lax.psum(partial_value[member], ("mp", "dp")) for member in range(members)], 0
    )
    losses = totals / entries
    return (losses, denoised_f.astype(jnp.bfloat16))


def solution(mesh):
    placed = (
        P("mp", "dp"),
        P("mp", "dp"),
        P("dp"),
        P("cand", None, "mp", None),
        P("cand", None, "mp", None),
        P("cand", None),
        P("cand", None),
    )
    return jax.shard_map(
        on_device,
        mesh=mesh,
        in_specs=placed,
        out_specs=(P("cand"), P("cand", "mp", "dp")),
        check_vma=False,
    )
```

profile of v0, /device:TPU:0, one launch (start us, length us, event | category | flops | bytes accessed | tf_op | source)
XLA Modules:
  0.0 995.8 jit_solution(4522708528994978643)
XLA Ops:
  7.2 0.8 select_reduce_fusion
  10.0 1.8 fusion.63
  12.7 361.6 %while.33 = (s32[]{:T(128)}, f32[2,9,192,1536]{3,2,1,0:T(8,128)}, f32[2,9,192,1536]{3,2,1,0:T(8,128)}, s32[]{:T(128)}, f32[2,16]{0,1:T(8,128)S(1)}, /*index=5*/b...) while((s32[]{:T(128)}, f32[2,9,192,1536]{3,2,1,0:T(8,128)}, ...), condition=%wide.region_4.5_spmd.clone, body=%wide.region_3.4_spmd.clone.sunk | while | flops 37158920 | bytes 138019008 | solution.py:62
  12.7 11.6 %bitcast_convert_fusion.7 = (f32[9,192,1536]{2,1,0:T(8,128)}, f32[9,192,1536]{2,1,0:T(8,128)}) fusion(bf16[8,9,192,1536]{3,2,1,0:T(8,128)(2,1)} %get-tuple-element.524, s32[]{:T(128)S(6)} %copy.24, bf16[8,9,192,1536]{3,2,1,0:T(8,128)(2,1)} %get-tuple-element.523), kind=kLoop, calls=%fused_computation.8.clone.1 | loop fusion | flops 5308416 | bytes 31850500 | tf_op jit(solution)/shard_map/while/body/eval_jaxpr/mul | solution.py:59
  24.3 23.7 %select_add_fusion.7 = (f32[2,9,192,1536]{3,2,1,0:T(8,128)}, f32[2,9,192,1536]{3,2,1,0:T(8,128)}) fusion(f32[2,9,192,1536]{3,2,1,0:T(8,128)} %get-tuple-element.510, f32[9,192,1536]{2,1,0:T(8,128)} %get-tuple-element.464, f32[2]{0:T(128)S(1)} %fusion.75, pred[]{:T(512)S(6)} %compare.13, f32[9,192,1536]{2,1,0:T(8,128)} %get-tuple-element.465, ...), kind=kLoop, calls=%fused_computation.6.clone.1 | loop fusion | flops 31850496 | bytes 106168328 | tf_op jit(solution)/shard_map/while/body/eval_jaxpr/add | solution.py:59
  48.0 11.6 %bitcast_convert_fusion.7 = (f32[9,192,1536]{2,1,0:T(8,128)}, f32[9,192,1536]{2,1,0:T(8,128)}) fusion(bf16[8,9,192,1536]{3,2,1,0:T(8,128)(2,1)} %get-tuple-element.524, s32[]{:T(128)S(6)} %copy.24, bf16[8,9,192,1536]{3,2,1,0:T(8,128)(2,1)} %get-tuple-element.523), kind=kLoop, calls=%fused_computation.8.clone.1 | loop fusion | flops 5308416 | bytes 31850500 | tf_op jit(solution)/shard_map/while/body/eval_jaxpr/mul | solution.py:59
  59.6 35.0 %select_add_fusion.7 = (f32[2,9,192,1536]{3,2,1,0:T(8,128)}, f32[2,9,192,1536]{3,2,1,0:T(8,128)}) fusion(f32[2,9,192,1536]{3,2,1,0:T(8,128)} %get-tuple-element.510, f32[9,192,1536]{2,1,0:T(8,128)} %get-tuple-element.464, f32[2]{0:T(128)S(1)} %fusion.75, pred[]{:T(512)S(6)} %compare.13, f32[9,192,1536]{2,1,0:T(8,128)} %get-tuple-element.465, ...), kind=kLoop, calls=%fused_computation.6.clone.1 | loop fusion | flops 31850496 | bytes 106168328 | tf_op jit(solution)/shard_map/while/body/eval_jaxpr/add | solution.py:59
  94.6 11.5 %bitcast_convert_fusion.7 = (f32[9,192,1536]{2,1,0:T(8,128)}, f32[9,192,1536]{2,1,0:T(8,128)}) fusion(bf16[8,9,192,1536]{3,2,1,0:T(8,128)(2,1)} %get-tuple-element.524, s32[]{:T(128)S(6)} %copy.24, bf16[8,9,192,1536]{3,2,1,0:T(8,128)(2,1)} %get-tuple-element.523), kind=kLoop, calls=%fused_computation.8.clone.1 | loop fusion | flops 5308416 | bytes 31850500 | tf_op jit(solution)/shard_map/while/body/eval_jaxpr/mul | solution.py:59
  106.2 35.0 %select_add_fusion.7 = (f32[2,9,192,1536]{3,2,1,0:T(8,128)}, f32[2,9,192,1536]{3,2,1,0:T(8,128)}) fusion(f32[2,9,192,1536]{3,2,1,0:T(8,128)} %get-tuple-element.510, f32[9,192,1536]{2,1,0:T(8,128)} %get-tuple-element.464, f32[2]{0:T(128)S(1)} %fusion.75, pred[]{:T(512)S(6)} %compare.13, f32[9,192,1536]{2,1,0:T(8,128)} %get-tuple-element.465, ...), kind=kLoop, calls=%fused_computation.6.clone.1 | loop fusion | flops 31850496 | bytes 106168328 | tf_op jit(solution)/shard_map/while/body/eval_jaxpr/add | solution.py:59
  141.2 11.5 %bitcast_convert_fusion.7 = (f32[9,192,1536]{2,1,0:T(8,128)}, f32[9,192,1536]{2,1,0:T(8,128)}) fusion(bf16[8,9,192,1536]{3,2,1,0:T(8,128)(2,1)} %get-tuple-element.524, s32[]{:T(128)S(6)} %copy.24, bf16[8,9,192,1536]{3,2,1,0:T(8,128)(2,1)} %get-tuple-element.523), kind=kLoop, calls=%fused_computation.8.clone.1 | loop fusion | flops 5308416 | bytes 31850500 | tf_op jit(solution)/shard_map/while/body/eval_jaxpr/mul | solution.py:59
  152.8 35.0 %select_add_fusion.7 = (f32[2,9,192,1536]{3,2,1,0:T(8,128)}, f32[2,9,192,1536]{3,2,1,0:T(8,128)}) fusion(f32[2,9,192,1536]{3,2,1,0:T(8,128)} %get-tuple-element.510, f32[9,192,1536]{2,1,0:T(8,128)} %get-tuple-element.464, f32[2]{0:T(128)S(1)} %fusion.75, pred[]{:T(512)S(6)} %compare.13, f32[9,192,1536]{2,1,0:T(8,128)} %get-tuple-element.465, ...), kind=kLoop, calls=%fused_computation.6.clone.1 | loop fusion | flops 31850496 | bytes 106168328 | tf_op jit(solution)/shard_map/while/body/eval_jaxpr/add | solution.py:59
  187.8 11.5 %bitcast_convert_fusion.7 = (f32[9,192,1536]{2,1,0:T(8,128)}, f32[9,192,1536]{2,1,0:T(8,128)}) fusion(bf16[8,9,192,1536]{3,2,1,0:T(8,128)(2,1)} %get-tuple-element.524, s32[]{:T(128)S(6)} %copy.24, bf16[8,9,192,1536]{3,2,1,0:T(8,128)(2,1)} %get-tuple-element.523), kind=kLoop, calls=%fused_computation.8.clone.1 | loop fusion | flops 5308416 | bytes 31850500 | tf_op jit(solution)/shard_map/while/body/eval_jaxpr/mul | solution.py:59
  199.4 35.0 %select_add_fusion.7 = (f32[2,9,192,1536]{3,2,1,0:T(8,128)}, f32[2,9,192,1536]{3,2,1,0:T(8,128)}) fusion(f32[2,9,192,1536]{3,2,1,0:T(8,128)} %get-tuple-element.510, f32[9,192,1536]{2,1,0:T(8,128)} %get-tuple-element.464, f32[2]{0:T(128)S(1)} %fusion.75, pred[]{:T(512)S(6)} %compare.13, f32[9,192,1536]{2,1,0:T(8,128)} %get-tuple-element.465, ...), kind=kLoop, calls=%fused_computation.6.clone.1 | loop fusion | flops 31850496 | bytes 106168328 | tf_op jit(solution)/shard_map/while/body/eval_jaxpr/add | solution.py:59
  234.4 11.5 %bitcast_convert_fusion.7 = (f32[9,192,1536]{2,1,0:T(8,128)}, f32[9,192,1536]{2,1,0:T(8,128)}) fusion(bf16[8,9,192,1536]{3,2,1,0:T(8,128)(2,1)} %get-tuple-element.524, s32[]{:T(128)S(6)} %copy.24, bf16[8,9,192,1536]{3,2,1,0:T(8,128)(2,1)} %get-tuple-element.523), kind=kLoop, calls=%fused_computation.8.clone.1 | loop fusion | flops 5308416 | bytes 31850500 | tf_op jit(solution)/shard_map/while/body/eval_jaxpr/mul | solution.py:59
  246.0 35.0 %select_add_fusion.7 = (f32[2,9,192,1536]{3,2,1,0:T(8,128)}, f32[2,9,192,1536]{3,2,1,0:T(8,128)}) fusion(f32[2,9,192,1536]{3,2,1,0:T(8,128)} %get-tuple-element.510, f32[9,192,1536]{2,1,0:T(8,128)} %get-tuple-element.464, f32[2]{0:T(128)S(1)} %fusion.75, pred[]{:T(512)S(6)} %compare.13, f32[9,192,1536]{2,1,0:T(8,128)} %get-tuple-element.465, ...), kind=kLoop, calls=%fused_computation.6.clone.1 | loop fusion | flops 31850496 | bytes 106168328 | tf_op jit(solution)/shard_map/while/body/eval_jaxpr/add | solution.py:59
  281.0 11.5 %bitcast_convert_fusion.7 = (f32[9,192,1536]{2,1,0:T(8,128)}, f32[9,192,1536]{2,1,0:T(8,128)}) fusion(bf16[8,9,192,1536]{3,2,1,0:T(8,128)(2,1)} %get-tuple-element.524, s32[]{:T(128)S(6)} %copy.24, bf16[8,9,192,1536]{3,2,1,0:T(8,128)(2,1)} %get-tuple-element.523), kind=kLoop, calls=%fused_computation.8.clone.1 | loop fusion | flops 5308416 | bytes 31850500 | tf_op jit(solution)/shard_map/while/body/eval_jaxpr/mul | solution.py:59
  292.6 35.0 %select_add_fusion.7 = (f32[2,9,192,1536]{3,2,1,0:T(8,128)}, f32[2,9,192,1536]{3,2,1,0:T(8,128)}) fusion(f32[2,9,192,1536]{3,2,1,0:T(8,128)} %get-tuple-element.510, f32[9,192,1536]{2,1,0:T(8,128)} %get-tuple-element.464, f32[2]{0:T(128)S(1)} %fusion.75, pred[]{:T(512)S(6)} %compare.13, f32[9,192,1536]{2,1,0:T(8,128)} %get-tuple-element.465, ...), kind=kLoop, calls=%fused_computation.6.clone.1 | loop fusion | flops 31850496 | bytes 106168328 | tf_op jit(solution)/shard_map/while/body/eval_jaxpr/add | solution.py:59
  327.6 11.5 %bitcast_convert_fusion.7 = (f32[9,192,1536]{2,1,0:T(8,128)}, f32[9,192,1536]{2,1,0:T(8,128)}) fusion(bf16[8,9,192,1536]{3,2,1,0:T(8,128)(2,1)} %get-tuple-element.524, s32[]{:T(128)S(6)} %copy.24, bf16[8,9,192,1536]{3,2,1,0:T(8,128)(2,1)} %get-tuple-element.523), kind=kLoop, calls=%fused_computation.8.clone.1 | loop fusion | flops 5308416 | bytes 31850500 | tf_op jit(solution)/shard_map/while/body/eval_jaxpr/mul | solution.py:59
  339.2 35.0 %select_add_fusion.7 = (f32[2,9,192,1536]{3,2,1,0:T(8,128)}, f32[2,9,192,1536]{3,2,1,0:T(8,128)}) fusion(f32[2,9,192,1536]{3,2,1,0:T(8,128)} %get-tuple-element.510, f32[9,192,1536]{2,1,0:T(8,128)} %get-tuple-element.464, f32[2]{0:T(128)S(1)} %fusion.75, pred[]{:T(512)S(6)} %compare.13, f32[9,192,1536]{2,1,0:T(8,128)} %get-tuple-element.465, ...), kind=kLoop, calls=%fused_computation.6.clone.1 | loop fusion | flops 31850496 | bytes 106168328 | tf_op jit(solution)/shard_map/while/body/eval_jaxpr/add | solution.py:59
  374.7 366.4 %while.32 = (s32[]{:T(128)}, f32[2,9,192,1536]{3,2,1,0:T(8,128)}, f32[2,9,192,1536]{3,2,1,0:T(8,128)}, s32[]{:T(128)}, f32[2,16]{0,1:T(8,128)}, /*index=5*/bf16[...) while((s32[]{:T(128)}, f32[2,9,192,1536]{3,2,1,0:T(8,128)}, ...), condition=%wide.region_2.3_spmd.clone, body=%wide.region_1.2_spmd.clone.sunk | while | flops 37158920 | bytes 138019008 | solution.py:62
  374.7 11.5 %bitcast_convert_fusion.6 = (f32[9,192,1536]{2,1,0:T(8,128)}, f32[9,192,1536]{2,1,0:T(8,128)}) fusion(bf16[8,9,192,1536]{3,2,1,0:T(8,128)(2,1)} %get-tuple-element.494, s32[]{:T(128)S(6)} %copy.15, bf16[8,9,192,1536]{3,2,1,0:T(8,128)(2,1)} %get-tuple-element.493), kind=kLoop, calls=%fused_computation.2.clone.1 | loop fusion | flops 5308416 | bytes 31850500 | tf_op jit(solution)/shard_map/while/body/eval_jaxpr/mul | solution.py:59
  386.3 0.7 fusion.74
  387.0 23.6 %select_add_fusion.6 = (f32[2,9,192,1536]{3,2,1,0:T(8,128)}, f32[2,9,192,1536]{3,2,1,0:T(8,128)}) fusion(f32[2,9,192,1536]{3,2,1,0:T(8,128)} %get-tuple-element.480, f32[9,192,1536]{2,1,0:T(8,128)} %get-tuple-element.453, f32[2]{0:T(128)S(1)} %fusion.74, pred[]{:T(512)S(6)} %compare.12, f32[9,192,1536]{2,1,0:T(8,128)} %get-tuple-element.454, ...), kind=kLoop, calls=%fused_computation.clone.1 | loop fusion | flops 31850496 | bytes 106168328 | tf_op jit(solution)/shard_map/while/body/eval_jaxpr/add | solution.py:59
  410.5 11.5 %bitcast_convert_fusion.6 = (f32[9,192,1536]{2,1,0:T(8,128)}, f32[9,192,1536]{2,1,0:T(8,128)}) fusion(bf16[8,9,192,1536]{3,2,1,0:T(8,128)(2,1)} %get-tuple-element.494, s32[]{:T(128)S(6)} %copy.15, bf16[8,9,192,1536]{3,2,1,0:T(8,128)(2,1)} %get-tuple-element.493), kind=kLoop, calls=%fused_computation.2.clone.1 | loop fusion | flops 5308416 | bytes 31850500 | tf_op jit(solution)/shard_map/while/body/eval_jaxpr/mul | solution.py:59
  422.1 0.7 fusion.74
  422.8 35.0 %select_add_fusion.6 = (f32[2,9,192,1536]{3,2,1,0:T(8,128)}, f32[2,9,192,1536]{3,2,1,0:T(8,128)}) fusion(f32[2,9,192,1536]{3,2,1,0:T(8,128)} %get-tuple-element.480, f32[9,192,1536]{2,1,0:T(8,128)} %get-tuple-element.453, f32[2]{0:T(128)S(1)} %fusion.74, pred[]{:T(512)S(6)} %compare.12, f32[9,192,1536]{2,1,0:T(8,128)} %get-tuple-element.454, ...), kind=kLoop, calls=%fused_computation.clone.1 | loop fusion | flops 31850496 | bytes 106168328 | tf_op jit(solution)/shard_map/while/body/eval_jaxpr/add | solution.py:59
  457.8 11.5 %bitcast_convert_fusion.6 = (f32[9,192,1536]{2,1,0:T(8,128)}, f32[9,192,1536]{2,1,0:T(8,128)}) fusion(bf16[8,9,192,1536]{3,2,1,0:T(8,128)(2,1)} %get-tuple-element.494, s32[]{:T(128)S(6)} %copy.15, bf16[8,9,192,1536]{3,2,1,0:T(8,128)(2,1)} %get-tuple-element.493), kind=kLoop, calls=%fused_computation.2.clone.1 | loop fusion | flops 5308416 | bytes 31850500 | tf_op jit(solution)/shard_map/while/body/eval_jaxpr/mul | solution.py:59
  469.3 0.7 fusion.74
  470.0 35.0 %select_add_fusion.6 = (f32[2,9,192,1536]{3,2,1,0:T(8,128)}, f32[2,9,192,1536]{3,2,1,0:T(8,128)}) fusion(f32[2,9,192,1536]{3,2,1,0:T(8,128)} %get-tuple-element.480, f32[9,192,1536]{2,1,0:T(8,128)} %get-tuple-element.453, f32[2]{0:T(128)S(1)} %fusion.74, pred[]{:T(512)S(6)} %compare.12, f32[9,192,1536]{2,1,0:T(8,128)} %get-tuple-element.454, ...), kind=kLoop, calls=%fused_computation.clone.1 | loop fusion | flops 31850496 | bytes 106168328 | tf_op jit(solution)/shard_map/while/body/eval_jaxpr/add | solution.py:59
  505.0 11.5 %bitcast_convert_fusion.6 = (f32[9,192,1536]{2,1,0:T(8,128)}, f32[9,192,1536]{2,1,0:T(8,128)}) fusion(bf16[8,9,192,1536]{3,2,1,0:T(8,128)(2,1)} %get-tuple-element.494, s32[]{:T(128)S(6)} %copy.15, bf16[8,9,192,1536]{3,2,1,0:T(8,128)(2,1)} %get-tuple-element.493), kind=kLoop, calls=%fused_computation.2.clone.1 | loop fusion | flops 5308416 | bytes 31850500 | tf_op jit(solution)/shard_map/while/body/eval_jaxpr/mul | solution.py:59
  516.5 0.7 fusion.74
  517.2 35.0 %select_add_fusion.6 = (f32[2,9,192,1536]{3,2,1,0:T(8,128)}, f32[2,9,192,1536]{3,2,1,0:T(8,128)}) fusion(f32[2,9,192,1536]{3,2,1,0:T(8,128)} %get-tuple-element.480, f32[9,192,1536]{2,1,0:T(8,128)} %get-tuple-element.453, f32[2]{0:T(128)S(1)} %fusion.74, pred[]{:T(512)S(6)} %compare.12, f32[9,192,1536]{2,1,0:T(8,128)} %get-tuple-element.454, ...), kind=kLoop, calls=%fused_computation.clone.1 | loop fusion | flops 31850496 | bytes 106168328 | tf_op jit(solution)/shard_map/while/body/eval_jaxpr/add | solution.py:59
  552.2 11.5 %bitcast_convert_fusion.6 = (f32[9,192,1536]{2,1,0:T(8,128)}, f32[9,192,1536]{2,1,0:T(8,128)}) fusion(bf16[8,9,192,1536]{3,2,1,0:T(8,128)(2,1)} %get-tuple-element.494, s32[]{:T(128)S(6)} %copy.15, bf16[8,9,192,1536]{3,2,1,0:T(8,128)(2,1)} %get-tuple-element.493), kind=kLoop, calls=%fused_computation.2.clone.1 | loop fusion | flops 5308416 | bytes 31850500 | tf_op jit(solution)/shard_map/while/body/eval_jaxpr/mul | solution.py:59
  563.8 0.7 fusion.74
  564.4 35.0 %select_add_fusion.6 = (f32[2,9,192,1536]{3,2,1,0:T(8,128)}, f32[2,9,192,1536]{3,2,1,0:T(8,128)}) fusion(f32[2,9,192,1536]{3,2,1,0:T(8,128)} %get-tuple-element.480, f32[9,192,1536]{2,1,0:T(8,128)} %get-tuple-element.453, f32[2]{0:T(128)S(1)} %fusion.74, pred[]{:T(512)S(6)} %compare.12, f32[9,192,1536]{2,1,0:T(8,128)} %get-tuple-element.454, ...), kind=kLoop, calls=%fused_computation.clone.1 | loop fusion | flops 31850496 | bytes 106168328 | tf_op jit(solution)/shard_map/while/body/eval_jaxpr/add | solution.py:59
  599.4 11.5 %bitcast_convert_fusion.6 = (f32[9,192,1536]{2,1,0:T(8,128)}, f32[9,192,1536]{2,1,0:T(8,128)}) fusion(bf16[8,9,192,1536]{3,2,1,0:T(8,128)(2,1)} %get-tuple-element.494, s32[]{:T(128)S(6)} %copy.15, bf16[8,9,192,1536]{3,2,1,0:T(8,128)(2,1)} %get-tuple-element.493), kind=kLoop, calls=%fused_computation.2.clone.1 | loop fusion | flops 5308416 | bytes 31850500 | tf_op jit(solution)/shard_map/while/body/eval_jaxpr/mul | solution.py:59
  611.0 0.7 fusion.74
  611.7 35.0 %select_add_fusion.6 = (f32[2,9,192,1536]{3,2,1,0:T(8,128)}, f32[2,9,192,1536]{3,2,1,0:T(8,128)}) fusion(f32[2,9,192,1536]{3,2,1,0:T(8,128)} %get-tuple-element.480, f32[9,192,1536]{2,1,0:T(8,128)} %get-tuple-element.453, f32[2]{0:T(128)S(1)} %fusion.74, pred[]{:T(512)S(6)} %compare.12, f32[9,192,1536]{2,1,0:T(8,128)} %get-tuple-element.454, ...), kind=kLoop, calls=%fused_computation.clone.1 | loop fusion | flops 31850496 | bytes 106168328 | tf_op jit(solution)/shard_map/while/body/eval_jaxpr/add | solution.py:59
  646.7 11.5 %bitcast_convert_fusion.6 = (f32[9,192,1536]{2,1,0:T(8,128)}, f32[9,192,1536]{2,1,0:T(8,128)}) fusion(bf16[8,9,192,1536]{3,2,1,0:T(8,128)(2,1)} %get-tuple-element.494, s32[]{:T(128)S(6)} %copy.15, bf16[8,9,192,1536]{3,2,1,0:T(8,128)(2,1)} %get-tuple-element.493), kind=kLoop, calls=%fused_computation.2.clone.1 | loop fusion | flops 5308416 | bytes 31850500 | tf_op jit(solution)/shard_map/while/body/eval_jaxpr/mul | solution.py:59
  658.2 0.7 fusion.74
  658.9 35.0 %select_add_fusion.6 = (f32[2,9,192,1536]{3,2,1,0:T(8,128)}, f32[2,9,192,1536]{3,2,1,0:T(8,128)}) fusion(f32[2,9,192,1536]{3,2,1,0:T(8,128)} %get-tuple-element.480, f32[9,192,1536]{2,1,0:T(8,128)} %get-tuple-element.453, f32[2]{0:T(128)S(1)} %fusion.74, pred[]{:T(512)S(6)} %compare.12, f32[9,192,1536]{2,1,0:T(8,128)} %get-tuple-element.454, ...), kind=kLoop, calls=%fused_computation.clone.1 | loop fusion | flops 31850496 | bytes 106168328 | tf_op jit(solution)/shard_map/while/body/eval_jaxpr/add | solution.py:59
  693.9 11.5 %bitcast_convert_fusion.6 = (f32[9,192,1536]{2,1,0:T(8,128)}, f32[9,192,1536]{2,1,0:T(8,128)}) fusion(bf16[8,9,192,1536]{3,2,1,0:T(8,128)(2,1)} %get-tuple-element.494, s32[]{:T(128)S(6)} %copy.15, bf16[8,9,192,1536]{3,2,1,0:T(8,128)(2,1)} %get-tuple-element.493), kind=kLoop, calls=%fused_computation.2.clone.1 | loop fusion | flops 5308416 | bytes 31850500 | tf_op jit(solution)/shard_map/while/body/eval_jaxpr/mul | solution.py:59
  705.4 0.7 fusion.74
  706.1 35.0 %select_add_fusion.6 = (f32[2,9,192,1536]{3,2,1,0:T(8,128)}, f32[2,9,192,1536]{3,2,1,0:T(8,128)}) fusion(f32[2,9,192,1536]{3,2,1,0:T(8,128)} %get-tuple-element.480, f32[9,192,1536]{2,1,0:T(8,128)} %get-tuple-element.453, f32[2]{0:T(128)S(1)} %fusion.74, pred[]{:T(512)S(6)} %compare.12, f32[9,192,1536]{2,1,0:T(8,128)} %get-tuple-element.454, ...), kind=kLoop, calls=%fused_computation.clone.1 | loop fusion | flops 31850496 | bytes 106168328 | tf_op jit(solution)/shard_map/while/body/eval_jaxpr/add | solution.py:59
  741.3 1.8 fusion.13
  743.2 1.8 fusion.16
  745.0 1.8 fusion.19
  746.8 1.8 fusion.22
  748.7 1.6 bitcast_dynamic-update-slice_fusion
  750.3 0.7 fusion.25
  751.0 0.7 fusion.28
  751.7 0.7 fusion.31
  752.3 0.7 fusion.34
  753.1 3.9 copy-done.1
  756.9 19.3 %multiply_convert_fusion = bf16[2,192,384]{2,1,0:T(8,128)(2,1)S(1)} fusion(bf16[9,1536,384]{2,1,0:T(8,128)(2,1)} %copy-done.1, f32[2,9,192,1536]{3,2,1,0:T(8,128)} %get-tuple-element.254, f32[2,9,192,1536]{3,2,1,0:T(8,128)} %collective-permute-done.2), kind=kOutput, calls=%fused_computation.61 | convolution fusion | flops 4088217600 | bytes 53379072 | tf_op jit(solution)/shard_map/gkoc,kct->got/dot_general | solution.py:90
  777.7 13.9 %add_convert_fusion.1 = bf16[2,9,192,1536]{3,2,1,0:T(8,128)(2,1)S(1)} fusion(f32[2,9,192,1536]{3,2,1,0:T(8,128)} %get-tuple-element.252, f32[2,9,192,1536]{3,2,1,0:T(8,128)} %collective-permute-done.1), kind=kLoop, calls=%fused_computation.13 | loop fusion | flops 10616832 | bytes 53084160 | tf_op jit(solution)/shard_map/convert_element_type | solution.py:89
  791.7 4.0 copy-done.2
  795.7 4.6 fusion.7
  800.4 7.0 fusion.6
  807.5 64.9 %reduce-scatter.5.cloned.1.call-done = f32[192,384]{1,0:T(8,128)} async-done(((f32[1536,384]{1,0:T(8,128)}), f32[192,384]{1,0:T(8,128)}) %reduce-scatter.5.cloned.1.call-update) | async-done | bytes 294928 | tf_op jit(solution)/shard_map/reduce_scatter | solution.py:97
  872.4 72.4 %reduce-scatter.3.cloned.1.call-done = f32[192,384]{1,0:T(8,128)} async-done(((f32[1536,384]{1,0:T(8,128)}), f32[192,384]{1,0:T(8,128)}) %reduce-scatter.3.cloned.1.call-update) | async-done | bytes 294928 | tf_op jit(solution)/shard_map/reduce_scatter | solution.py:97
  944.7 1.9 fusion.38
  947.3 40.2 %all-reduce.2 = (f32[1]{0:T(128)}, f32[1]{0:T(128)}) all-reduce(f32[1]{0:T(128)} %get-tuple-element.365, f32[1]{0:T(128)} %get-tuple-element.364), channel_id=1, replica_groups=mesh['cand'=2,'mp'=8,'dp'=2] {'mp','dp'}, use_global_device_ids=true, to_apply=%region_9.10 | all-reduce | flops 2 | bytes 16 | tf_op jit(solution)/shard_map/psum | solution.py:113
  987.5 1.8 maximum_multiply_fusion.1
  (63 shorter events, 5.7 us)
Async XLA Ops:
  7.2 734.1 %all-gather.2.cloned.1.call-start = ((), (), s32[]{:S(2)}) async-start(), calls=%async_computation.2 | async-start | bytes 1327104 | tf_op jit(solution)/shard_map/all_gather | solution.py:75
  8.0 4.6 collective-permute-start
  11.8 860.6 %reduce-scatter.5.cloned.1.call-start = ((), (), s32[]{:S(2)}) async-start(), calls=%async_computation.4 | async-start | bytes 2654208 | tf_op jit(solution)/shard_map/reduce_scatter | solution.py:97
  374.2 403.5 %collective-permute-start.1 = (f32[2,9,192,1536]{3,2,1,0:T(8,128)}, f32[2,9,192,1536]{3,2,1,0:T(8,128)}, u32[]{:S(2)}, u32[]{:S(2)}) collective-permute-start(f32[2,9,192,1536]{3,2,1,0:T(8,128)} %get-tuple-element.253), channel_id=1, source_target_pairs={{0,16},{16,0},{1,17},{17,1},{2,18},{18,2},{3,19},{19,3},{4,20},{20... | collective-permute-start | bytes 63701000 | tf_op jit(solution)/shard_map/ppermute | solution.py:13
  374.2 378.8 %collective-permute-start.2 = (f32[2,9,192,1536]{3,2,1,0:T(8,128)}, f32[2,9,192,1536]{3,2,1,0:T(8,128)}, u32[]{:S(2)}, u32[]{:S(2)}) collective-permute-start(f32[2,9,192,1536]{3,2,1,0:T(8,128)} %get-tuple-element.255), channel_id=1, source_target_pairs={{0,16},{16,0},{1,17},{17,1},{2,18},{18,2},{3,19},{19,3},{4,20},{20... | collective-permute-start | bytes 63701000 | tf_op jit(solution)/shard_map/ppermute | solution.py:13
  741.3 9.0 copy-start
  753.0 3.9 copy-start.1
  791.6 4.1 copy-start.2
  800.3 7.1 copy-start.4
  800.3 144.4 %copy-start.3 = (f32[192,384]{1,0:T(8,128)S(1)}, f32[192,384]{1,0:T(8,128)}, u32[]{:S(2)}) copy-start(f32[192,384]{1,0:T(8,128)} %get-tuple-element.358) | copy-start | bytes 884740
  800.3 144.4 %copy-start.5 = (f32[384]{0:T(512)S(1)}, f32[384]{0:T(512)}, u32[]{:S(2)}) copy-start(f32[384]{0:T(512)} %get-tuple-element.360) | copy-start | bytes 4612
  800.3 144.4 %copy-start.6 = (f32[384]{0:T(512)S(1)}, f32[384]{0:T(512)}, u32[]{:S(2)}) copy-start(f32[384]{0:T(512)} %get-tuple-element.362) | copy-start | bytes 4612
  800.3 144.4 %reduce-scatter.3.cloned.1.call-start = ((), (), s32[]{:S(2)}) async-start(), calls=%async_computation.3 | async-start | bytes 2654208 | tf_op jit(solution)/shard_map/reduce_scatter | solution.py:97
Sparse Core Ops, SparseCore 0:
  11.9 43.4 all-gather.1
  800.4 71.9 reduce-scatter.4
  875.9 68.8 reduce-scatter.2
where the time goes:
time: 996 us
  other arithmetic  757 us (76%)
  waiting for transfers between devices  137 us (14%)
  blocking collectives  40.2 us (4%)
  matrix products  30.9 us (3%)
  local copies, waits for them, and re-layouts  15 us (2%)
  between operations  14 us (1%)
    add x16, other arithmetic, accumulate(): totals[1] + coeff * second_snap[None]  538 us
    mul x16, other arithmetic, accumulate(): coeff * second_snap[None]  185 us
    reduce_scatter x2, waiting for transfers between devices, member_feature(): lax.psum_scatter(jnp.einsum('kio,kit->ot', w_part, h_stack[:, member], pr...  137 us
    psum x1, blocking collectives, on_device(): lax.psum(partial_value[member], ('mp', 'dp'))  40.2 us
  transfers between devices with their start and end apart: 6, of which 2 were waited for; matrix products, arithmetic and copies ran while one was open for 77% of the time, Pallas kernels for 0%

commit v1 on v0

v1 whole, which is shorter than its diff:
```python
import functools

import jax
import jax.numpy as jnp
from jax import lax
from jax.experimental import pallas as pl
from jax.experimental.pallas import tpu as pltpu
from jax.sharding import PartitionSpec as P

LEVELS = 32
SIGMA_DATA = 0.5
MESH = pl.DeviceIdType.MESH


def from_partner(value, axis, apart):
    return lax.ppermute(value, axis, [(i, i ^ 1 << apart) for i in range(lax.axis_size(axis))])


def noise_scale(level_index):
    ratio = 2.0 * level_index.astype(jnp.float32) / (LEVELS - 1) - 1.0
    return jnp.exp(-0.4 + 2.0 * ratio)


def tap_matrix(tap):
    down_by, right_by = tap // 3 - 1, tap % 3 - 1
    source = lax.broadcasted_iota(jnp.int32, (128, 128), 0)
    target = lax.broadcasted_iota(jnp.int32, (128, 128), 1)
    row, col = (target & 63) >> 3, target & 7
    inside = (
        (row + down_by >= 0) & (row + down_by < 8) & (col + right_by >= 0) & (col + right_by < 8)
    )
    hit = (source == target + (down_by * 8 + right_by)) & inside
    return jnp.where(hit, 1.0, 0.0).astype(jnp.bfloat16)


def conv_kernel(
    taps, groups, mix_ref, x_ref, first_ref, second_ref, out_ref,
    give, mine, got, x_full, x_tap, pre, hidden,
    send_sem, recv_sem, x_send, x_recv,
):
    step = pl.program_id(0)
    chunks = 2 * taps
    snaps, rows, width = first_ref.shape[0], first_ref.shape[2], first_ref.shape[3]
    members, tokens = pre.shape[0], pre.shape[2]
    tiles = tokens // 128
    cand, me = lax.axis_index("cand"), lax.axis_index("mp")
    partner = 1 - cand
    block = 16 if rows % 16 == 0 else rows

    def exchange(chunk):
        return pltpu.make_async_remote_copy(
            src_ref=give.at[chunk % 2],
            dst_ref=got.at[chunk % 4],
            send_sem=send_sem.at[chunk % 2],
            recv_sem=recv_sem.at[chunk % 4],
            device_id={"cand": partner},
            device_id_type=MESH,
        )

    def x_copy(away, slot):
        return pltpu.make_async_remote_copy(
            src_ref=x_ref,
            dst_ref=x_full.at[slot],
            send_sem=x_send.at[away],
            recv_sem=x_recv.at[away],
            device_id={"mp": (me + away) % groups},
            device_id_type=MESH,
        )

    @pl.when(step == 0)
    def _():
        barrier = pltpu.get_barrier_semaphore()
        pl.semaphore_signal(barrier, inc=1, device_id={"cand": partner}, device_id_type=MESH)
        for away in range(1, groups):
            pl.semaphore_signal(
                barrier, inc=1, device_id={"mp": (me + away) % groups}, device_id_type=MESH
            )
        pl.semaphore_wait(barrier, groups)
        for away in range(1, groups):
            x_copy(away, me).start()
        x_full[me] = x_ref[...]
        pre[...] = jnp.zeros_like(pre)
        out_ref[...] = jnp.zeros_like(out_ref)

    def blend(source):
        coeff = [[mix_ref[c, s] for s in range(snaps)] for c in range(2 * members)]
        slot = step % 2

        def body(which, carry):
            at = pl.ds(pl.multiple_of(which * block, block), block)
            for tile in range(width // 128):
                lanes = pl.ds(tile * 128, 128)
                totals = [None] * (2 * members)
                for s in range(snaps):
                    value = source[s, 0, at, lanes].astype(jnp.float32)
                    for c in range(2 * members):
                        term = coeff[c][s] * value
                        totals[c] = term if s == 0 else totals[c] + term
                for c in range(members):
                    mine[slot, c, at, lanes] = totals[c]
                    give[slot, c, at, lanes] = totals[members + c]
            return carry

        lax.fori_loop(0, rows // block, body, 0)

    @pl.when((step >= 2) & (step < chunks))
    def _():
        exchange(step - 2).wait_send()

    @pl.when(step < taps)
    def _():
        blend(first_ref)

    @pl.when((step >= taps) & (step < chunks))
    def _():
        blend(second_ref)

    @pl.when(step < chunks)
    def _():
        exchange(step).start()

    @pl.when(step == 1)
    def _():
        for away in range(1, groups):
            copy = x_copy(away, (me + groups - away) % groups)
            copy.wait_send()
            copy.wait_recv()

    done = step - 1

    @pl.when(step >= 1)
    def _():
        exchange(done).wait_recv()

    @pl.when((step >= 1) & (done < taps))
    def _():
        shift = tap_matrix(done)
        for group in range(groups):
            for tile in range(tiles):
                lanes = pl.ds(tile * 128, 128)
                x_tap[pl.ds(group * rows, rows), lanes] = jnp.dot(
                    x_full[group, :, lanes], shift, preferred_element_type=jnp.float32
                ).astype(jnp.bfloat16)
        for c in range(members):
            weight = (mine[done % 2, c] + got[done % 4, c]).astype(jnp.bfloat16)
            pre[c] += jnp.dot(weight, x_tap[...], preferred_element_type=jnp.float32)

    @pl.when(done == taps - 1)
    def _():
        value = pre[...]
        hidden[...] = (value * jax.nn.sigmoid(value)).astype(jnp.bfloat16)

    @pl.when((step >= 1) & (done >= taps))
    def _():
        shift = tap_matrix(done - taps)
        for c in range(members):
            shifted = jnp.concatenate(
                [
                    jnp.dot(
                        hidden[c, :, pl.ds(tile * 128, 128)],
                        shift,
                        preferred_element_type=jnp.float32,
                    ).astype(jnp.bfloat16)
                    for tile in range(tiles)
                ],
                axis=1,
            )
            for part in range(width // 256):
                lanes = pl.ds(part * 256, 256)
                weight = (mine[done % 2, c, :, lanes] + got[done % 4, c, :, lanes]).astype(
                    jnp.bfloat16
                )
                out_ref[lanes, pl.ds(c * tokens, tokens)] += lax.dot_general(
                    weight, shifted, (((0,), (0,)), ((), ())), preferred_element_type=jnp.float32
                )

    @pl.when(step == chunks)
    def _():
        exchange(chunks - 2).wait_send()
        exchange(chunks - 1).wait_send()


def convolve(mix, x_own, snap_first, snap_second, groups):
    snaps, taps, rows, width = snap_first.shape
    members, tokens = mix.shape[0] // 2, x_own.shape[1]
    pair = (members, rows, width)
    return pl.pallas_call(
        functools.partial(conv_kernel, taps, groups),
        grid=(2 * taps + 1,),
        out_shape=jax.ShapeDtypeStruct((width, members * tokens), jnp.float32),
        in_specs=[
            pl.BlockSpec(memory_space=pltpu.SMEM),
            pl.BlockSpec((rows, tokens), lambda i: (0, 0)),
            pl.BlockSpec((snaps, 1, rows, width), lambda i: (0, jnp.minimum(i, taps - 1), 0, 0)),
            pl.BlockSpec(
                (snaps, 1, rows, width), lambda i: (0, jnp.clip(i - taps, 0, taps - 1), 0, 0)
            ),
        ],
        out_specs=pl.BlockSpec((width, members * tokens), lambda i: (0, 0)),
        scratch_shapes=[
            pltpu.VMEM((2,) + pair, jnp.float32),
            pltpu.VMEM((2,) + pair, jnp.float32),
            pltpu.VMEM((4,) + pair, jnp.float32),
            pltpu.VMEM((groups, rows, tokens), jnp.bfloat16),
            pltpu.VMEM((width, tokens), jnp.bfloat16),
            pltpu.VMEM((members, rows, tokens), jnp.float32),
            pltpu.VMEM((members, rows, tokens), jnp.bfloat16),
            pltpu.SemaphoreType.DMA((2,)),
            pltpu.SemaphoreType.DMA((4,)),
            pltpu.SemaphoreType.DMA((groups,)),
            pltpu.SemaphoreType.DMA((groups,)),
        ],
        compiler_params=pltpu.CompilerParams(
            collective_id=0,
            has_side_effects=True,
            dimension_semantics=("arbitrary",),
            vmem_limit_bytes=64 * 1024 * 1024 - 65536,
        ),
        name="blend_convolve",
    )(mix, x_own, snap_first, snap_second)


def total_kernel(groups, images, own_ref, out_ref, held, send_sem, recv_sem):
    me = lax.axis_index("mp") * images + lax.axis_index("dp")
    peers = groups * images

    def copy(away):
        to = (me + away) % peers
        return pltpu.make_async_remote_copy(
            src_ref=own_ref,
            dst_ref=held.at[away],
            send_sem=send_sem.at[away],
            recv_sem=recv_sem.at[away],
            device_id={"mp": to // images, "dp": to % images},
            device_id_type=MESH,
        )

    barrier = pltpu.get_barrier_semaphore()
    for away in range(1, peers):
        to = (me + away) % peers
        pl.semaphore_signal(
            barrier,
            inc=1,
            device_id={"mp": to // images, "dp": to % images},
            device_id_type=MESH,
        )
    pl.semaphore_wait(barrier, peers - 1)
    for away in range(1, peers):
        copy(away).start()
    total = own_ref[...]
    for away in range(1, peers):
        copy(away).wait_recv()
        total = total + held[away]
    out_ref[...] = total
    for away in range(1, peers):
        copy(away).wait_send()


def total_over(partial, groups, images):
    peers = groups * images
    return pl.pallas_call(
        functools.partial(total_kernel, groups, images),
        out_shape=jax.ShapeDtypeStruct(partial.shape, jnp.float32),
        in_specs=[pl.BlockSpec(memory_space=pltpu.VMEM)],
        out_specs=pl.BlockSpec(memory_space=pltpu.VMEM),
        scratch_shapes=[
            pltpu.VMEM((peers,) + partial.shape, jnp.float32),
            pltpu.SemaphoreType.DMA((peers,)),
            pltpu.SemaphoreType.DMA((peers,)),
        ],
        compiler_params=pltpu.CompilerParams(collective_id=1, has_side_effects=True),
        name="loss_total",
    )(partial)


def on_device(clean, noise, level_index, snap_first, snap_second, blend, snap_index):
    sigmas = jnp.repeat(noise_scale(level_index), 64)
    spread = sigmas * sigmas + SIGMA_DATA * SIGMA_DATA
    scale_in = 1.0 / jnp.sqrt(spread)
    scale_skip = SIGMA_DATA * SIGMA_DATA / spread
    scale_out = sigmas * SIGMA_DATA / jnp.sqrt(spread)
    weighting = spread / (sigmas * SIGMA_DATA) ** 2
    clean_f = clean.astype(jnp.float32)
    noisy = clean_f + sigmas * noise.astype(jnp.float32)
    x_own = (scale_in * noisy).astype(jnp.bfloat16)
    owned = snap_first.shape[0]
    stored = owned * lax.axis_size("cand")
    groups, images = lax.axis_size("mp"), lax.axis_size("dp")
    onehot = (snap_index[:, :, None] == jnp.arange(stored, dtype=jnp.int32)[None, None, :]).astype(
        jnp.float32
    )
    mixing = jnp.sum(blend[:, :, None] * onehot, 1)
    other_mix = from_partner(mixing, "cand", 0)
    first_slot = lax.axis_index("cand") * owned
    mix = lax.dynamic_slice_in_dim(jnp.concatenate([mixing, other_mix], 0), first_slot, owned, 1)
    members = blend.shape[0]
    sums = convolve(mix, x_own, snap_first, snap_second, groups)
    feature = lax.psum_scatter(sums, "mp", scatter_dimension=0, tiled=True)
    tokens = clean.shape[1]
    features = jnp.stack([feature[:, c * tokens : (c + 1) * tokens] for c in range(members)], 0)
    denoised_f = scale_skip[None, None, :] * noisy[None] + scale_out[None, None, :] * features
    partial_value = jnp.sum(
        weighting[None, None, :] * (denoised_f - clean_f[None]) ** 2, axis=(1, 2)
    )
    entries = clean.shape[0] * groups * clean.shape[1] * images
    tile = jnp.broadcast_to(jnp.pad(partial_value, (0, 8 - members))[:, None], (8, 128))
    losses = total_over(tile, groups, images)[:members, 0] / entries
    return (losses, denoised_f.astype(jnp.bfloat16))


def solution(mesh):
    placed = (
        P("mp", "dp"),
        P("mp", "dp"),
        P("dp"),
        P("cand", None, "mp", None),
        P("cand", None, "mp", None),
        P("cand", None),
        P("cand", None),
    )
    return jax.shard_map(
        on_device,
        mesh=mesh,
        in_specs=placed,
        out_specs=(P("cand"), P("cand", "mp", "dp")),
        check_vma=False,
    )
```

time: 996 us -> 241 us (0.24)
  other arithmetic: 757 us -> 7.93 us
  Pallas kernels: 0 us -> 113 us
  blocking collectives: 40.2 us -> 0 us
  waiting for transfers between devices: 137 us -> 103 us
  matrix products: 30.9 us -> 0 us
  local copies, waits for them, and re-layouts: 15 us -> 2.55 us
    add x16 -> x0, other arithmetic: 538 us -> none  [accumulate(): totals[1] + coeff * second_snap[None]]
    mul x16 -> x0, other arithmetic: 185 us -> none  [accumulate(): coeff * second_snap[None]]
    pallas_call x0 -> x2, Pallas kernels: none -> 113 us  [the longest x1 104 us: convolve(): pl.pallas_call(functools.partial(conv_kernel, taps, groups), grid=(2 * ta...]
    psum x1 -> x0, blocking collectives: 40.2 us -> none  [on_device(): lax.psum(partial_value[member], ('mp', 'dp'))]
    reduce_scatter x2 -> x1, waiting for transfers between devices: 137 us -> 103 us  [on_device(): feature = lax.psum_scatter(sums, 'mp', scatter_dimension=0, tiled=True)]
    dot_general x3 -> x0, matrix products: 30.9 us -> none  [the longest x1 19.3 us: on_device(): jnp.einsum('gkoc,kct->got', first_w, x_stack, preferred_element_type=jnp....]
    convert_element_type x1 -> x0, other arithmetic: 13.9 us -> none  [on_device(): second_w = (mine_second + got_second).astype(jnp.bfloat16)]
    unnamed x20 -> x0, other arithmetic: 12.2 us -> none
  transfers between devices with their start and end apart: 6 -> 2, of which waited for: 2 -> 1; matrix products, arithmetic and copies ran while one was open for 77% -> 2% of each run, Pallas kernels for 0% -> 0%
where the time goes in v1:
time: 241 us
  Pallas kernels  113 us (47%)
  waiting for transfers between devices  103 us (43%)
  between operations  14.1 us (6%)
  other arithmetic  7.93 us (3%)
  local copies, waits for them, and re-layouts  2.55 us (1%)
    pallas_call x1, Pallas kernels, convolve(): pl.pallas_call(functools.partial(conv_kernel, taps, groups), grid=(2 * ta...  104 us
    reduce_scatter x1, waiting for transfers between devices, on_device(): feature = lax.psum_scatter(sums, 'mp', scatter_dimension=0, tiled=True)  103 us
    pallas_call x1, Pallas kernels, total_over(): pl.pallas_call(functools.partial(total_kernel, groups, images), out_shape...  9.03 us
  transfers between devices with their start and end apart: 2, of which 1 were waited for; matrix products, arithmetic and copies ran while one was open for 2% of the time, Pallas kernels for 0%

profile of v1, /device:TPU:0, one launch (start us, length us, event | category | flops | bytes accessed | tf_op | source)
XLA Modules:
  0.0 240.6 jit_solution(6984853061137247215)
XLA Ops:
  7.2 0.0 reduce-scatter.2.cloned.1.call-start
  7.2 0.8 select_reduce_fusion
  8.0 0.6 collective-permute-start
  8.5 0.7 add_exponential_fusion
  9.2 0.1 broadcast_in_dim.4
  9.3 0.1 reshape.48
  9.4 0.6 multiply_divide_fusion
  10.0 1.8 fusion.2
  11.8 0.0 collective-permute-done
  11.8 0.6 constant_dynamic-slice_fusion.mix_ref
  12.4 103.9 %blend_convolve.1 = f32[1536,768]{1,0:T(8,128)} custom-call(f32[4,8]{1,0:T(4,128)} %constant_dynamic-slice_fusion.mix_ref, bf16[192,384]{1,0:T(8,128)(2,1)} %get-tuple-element.7.x_ref, bf16[8,9,192,1536]{3,2,1,0:T(8,128)(2,1)} %first_ref.1, bf16[8,9,192,1536]{3,2,1,0:T(8,128)(2,1)} %second_ref.1), custom_call_target="tpu_custom_call" | custom-call | tf_op jit(solution)/shard_map/blend_convolve/pallas_call | solution.py:187
  116.3 0.0 reduce-scatter.2.cloned.1.call-update
  116.3 0.9 convert_element_type.19
  117.3 102.5 %reduce-scatter.2.cloned.1.call-done = f32[192,768]{1,0:T(8,128)} async-done(((f32[1536,768]{1,0:T(8,128)}), f32[192,768]{1,0:T(8,128)}) %reduce-scatter.2.cloned.1.call-update) | async-done | bytes 589840 | tf_op jit(solution)/shard_map/reduce_scatter | solution.py:298
  219.8 1.1 slice_bitcast_fusion.1
  220.9 1.8 fusion.1
  222.7 0.7 broadcast_in_dim.5.own_ref
  223.4 9.0 %loss_total.1 = f32[8,128]{1,0:T(8,128)} custom-call(f32[8,128]{1,0:T(8,128)} %broadcast_in_dim.5.own_ref), custom_call_target="tpu_custom_call" | custom-call | tf_op jit(solution)/shard_map/loss_total/pallas_call | solution.py:261
  232.4 1.3 multiply_reduce_fusion.1
  (2 shorter events, 0.0 us)
Async XLA Ops:
  7.2 212.6 %reduce-scatter.2.cloned.1.call-start = ((), (), s32[]{:S(2)}) async-start(), calls=%async_computation.1 | async-start | bytes 5308416 | tf_op jit(solution)/shard_map/reduce_scatter | solution.py:298
  8.0 3.8 %collective-permute-start = (f32[2,16]{1,0:T(2,128)S(1)}, f32[2,16]{1,0:T(2,128)S(1)}, u32[]{:S(2)}, u32[]{:S(2)}) collective-permute-start(f32[2,16]{1,0:T(2,128)S(1)} %select_reduce_fusion), channel_id=1, source_target_pairs={{0,16},{16,0},{1,17},{17,1},{2,18},{18,2},{3,19},{19,3},{4,20},{20... | collective-permute-start | bytes 392 | tf_op jit(solution)/shard_map/ppermute | solution.py:16
Sparse Core Ops, SparseCore 0:
  116.5 103.2 reduce-scatter.1

commit v2 on v1

--- a/solution.py
+++ b/solution.py
@@ -1,4 +1,5 @@
 import functools
+import math
 
 import jax
 import jax.numpy as jnp
@@ -34,23 +35,27 @@
 
 
 def conv_kernel(
-    taps, groups, mix_ref, x_ref, first_ref, second_ref, out_ref,
-    give, mine, got, x_full, x_tap, pre, hidden,
-    send_sem, recv_sem, x_send, x_recv,
+    taps, groups, span, few, mix_ref, x_ref, first_ref, second_ref, out_ref,
+    give, mine, got, x_full, x_tap, pre, hidden, sums, paired, landed,
+    send_sem, recv_sem, x_send, x_recv, pair_send, pair_recv, owner_send, owner_recv,
 ):
     step = pl.program_id(0)
-    chunks = 2 * taps
     snaps, rows, width = first_ref.shape[0], first_ref.shape[2], first_ref.shape[3]
     members, tokens = pre.shape[0], pre.shape[2]
     tiles = tokens // 128
+    pieces, parts = width // span, taps // few
+    chunks = taps + pieces * parts
+    pairs, couples = groups // 2, span // (2 * rows)
     cand, me = lax.axis_index("cand"), lax.axis_index("mp")
     partner = 1 - cand
+    side = me % 2
+    my_piece = me // (2 * couples)
     block = 16 if rows % 16 == 0 else rows
 
-    def exchange(chunk):
+    def exchange(chunk, count):
         return pltpu.make_async_remote_copy(
-            src_ref=give.at[chunk % 2],
-            dst_ref=got.at[chunk % 4],
+            src_ref=give.at[chunk % 2, :, pl.ds(0, count)],
+            dst_ref=got.at[chunk % 4, :, pl.ds(0, count)],
             send_sem=send_sem.at[chunk % 2],
             recv_sem=recv_sem.at[chunk % 4],
             device_id={"cand": partner},
@@ -66,6 +71,43 @@
             device_id={"mp": (me + away) % groups},
             device_id_type=MESH,
         )
+
+    def piece_of(stage):
+        return (my_piece + stage + 1) % pieces
+
+    def pair_copy(couple):
+        return pltpu.make_async_remote_copy(
+            src_ref=sums.at[2 * couple + 1 - side],
+            dst_ref=paired.at[couple],
+            send_sem=pair_send.at[couple],
+            recv_sem=pair_recv.at[couple],
+            device_id={"mp": me + 1 - 2 * side},
+            device_id_type=MESH,
+        )
+
+    def owner_copy(couple, slot):
+        return pltpu.make_async_remote_copy(
+            src_ref=paired.at[couple],
+            dst_ref=landed.at[slot],
+            send_sem=owner_send.at[couple],
+            recv_sem=owner_recv.at[slot],
+            device_id={"mp": 2 * couple + side},
+            device_id_type=MESH,
+        )
+
+    def start_pairs(stage):
+        for which in range(couples):
+            pair_copy(piece_of(stage) * couples + which).start()
+
+    def finish_pairs(stage):
+        for which in range(couples):
+            couple = piece_of(stage) * couples + which
+            pair_copy(couple).wait_recv()
+            paired[couple] = paired[couple] + sums[2 * couple + side]
+
+            @pl.when(couple != me // 2)
+            def _():
+                owner_copy(couple, me // 2).start()
 
     @pl.when(step == 0)
     def _():
@@ -80,44 +122,47 @@
             x_copy(away, me).start()
         x_full[me] = x_ref[...]
         pre[...] = jnp.zeros_like(pre)
-        out_ref[...] = jnp.zeros_like(out_ref)
-
-    def blend(source):
+
+    def blend(source, count, columns, place):
         coeff = [[mix_ref[c, s] for s in range(snaps)] for c in range(2 * members)]
         slot = step % 2
 
         def body(which, carry):
             at = pl.ds(pl.multiple_of(which * block, block), block)
-            for tile in range(width // 128):
-                lanes = pl.ds(tile * 128, 128)
-                totals = [None] * (2 * members)
-                for s in range(snaps):
-                    value = source[s, 0, at, lanes].astype(jnp.float32)
-                    for c in range(2 * members):
-                        term = coeff[c][s] * value
-                        totals[c] = term if s == 0 else totals[c] + term
-                for c in range(members):
-                    mine[slot, c, at, lanes] = totals[c]
-                    give[slot, c, at, lanes] = totals[members + c]
+            for tap in range(count):
+                for tile in range(columns // 128):
+                    lanes = pl.ds(tile * 128, 128)
+                    totals = [None] * (2 * members)
+                    for s in range(snaps):
+                        value = source[s, tap, at, lanes].astype(jnp.float32)
+                        for c in range(2 * members):
+                            term = coeff[c][s] * value
+                            totals[c] = term if s == 0 else totals[c] + term
+                    piece, first = place(tap, tile)
+                    for c in range(members):
+                        mine[slot, c, piece, at, pl.ds(first, 128)] = totals[c]
+                        give[slot, c, piece, at, pl.ds(first, 128)] = totals[members + c]
             return carry
 
         lax.fori_loop(0, rows // block, body, 0)
 
-    @pl.when((step >= 2) & (step < chunks))
-    def _():
-        exchange(step - 2).wait_send()
+    @pl.when((step >= 2) & (step < taps + 2))
+    def _():
+        exchange(step - 2, pieces).wait_send()
+
+    @pl.when((step >= taps + 2) & (step < chunks))
+    def _():
+        exchange(step - 2, few).wait_send()
 
     @pl.when(step < taps)
     def _():
-        blend(first_ref)
+        blend(first_ref, 1, width, lambda tap, tile: (tile * 128 // span, tile * 128 % span))
+        exchange(step, pieces).start()
 
     @pl.when((step >= taps) & (step < chunks))
     def _():
-        blend(second_ref)
-
-    @pl.when(step < chunks)
-    def _():
-        exchange(step).start()
+        blend(second_ref, few, span, lambda tap, tile: (tap, tile * 128))
+        exchange(step, few).start()
 
     @pl.when(step == 1)
     def _():
@@ -128,9 +173,8 @@
 
     done = step - 1
 
-    @pl.when(step >= 1)
-    def _():
-        exchange(done).wait_recv()
+    def weight_of(c, piece):
+        return (mine[done % 2, c, piece] + got[done % 4, c, piece]).astype(jnp.bfloat16)
 
     @pl.when((step >= 1) & (done < taps))
     def _():
@@ -141,8 +185,9 @@
                 x_tap[pl.ds(group * rows, rows), lanes] = jnp.dot(
                     x_full[group, :, lanes], shift, preferred_element_type=jnp.float32
                 ).astype(jnp.bfloat16)
+        exchange(done, pieces).wait_recv()
         for c in range(members):
-            weight = (mine[done % 2, c] + got[done % 4, c]).astype(jnp.bfloat16)
+            weight = jnp.concatenate([weight_of(c, piece) for piece in range(pieces)], axis=1)
             pre[c] += jnp.dot(weight, x_tap[...], preferred_element_type=jnp.float32)
 
     @pl.when(done == taps - 1)
@@ -152,63 +197,115 @@
 
     @pl.when((step >= 1) & (done >= taps))
     def _():
-        shift = tap_matrix(done - taps)
+        at = done - taps
+        stage, part = at // parts, at % parts
+        owners = piece_of(stage) * 2 * couples
+        shifts = [tap_matrix(part * few + tap) for tap in range(few)]
+        exchange(done, few).wait_recv()
         for c in range(members):
-            shifted = jnp.concatenate(
-                [
-                    jnp.dot(
-                        hidden[c, :, pl.ds(tile * 128, 128)],
-                        shift,
-                        preferred_element_type=jnp.float32,
-                    ).astype(jnp.bfloat16)
-                    for tile in range(tiles)
-                ],
-                axis=1,
+            moved = [
+                jnp.concatenate(
+                    [
+                        jnp.dot(
+                            hidden[c, :, pl.ds(tile * 128, 128)],
+                            shift,
+                            preferred_element_type=jnp.float32,
+                        ).astype(jnp.bfloat16)
+                        for tile in range(tiles)
+                    ],
+                    axis=1,
+                )
+                for shift in shifts
+            ]
+            weight = jnp.concatenate([weight_of(c, tap) for tap in range(few)], axis=0)
+            product = lax.dot_general(
+                weight,
+                jnp.concatenate(moved, axis=0),
+                (((0,), (0,)), ((), ())),
+                preferred_element_type=jnp.float32,
             )
-            for part in range(width // 256):
-                lanes = pl.ds(part * 256, 256)
-                weight = (mine[done % 2, c, :, lanes] + got[done % 4, c, :, lanes]).astype(
-                    jnp.bfloat16
-                )
-                out_ref[lanes, pl.ds(c * tokens, tokens)] += lax.dot_general(
-                    weight, shifted, (((0,), (0,)), ((), ())), preferred_element_type=jnp.float32
-                )
+            lanes = pl.ds(c * tokens, tokens)
+
+            @pl.when(part == 0)
+            def _():
+                for which in range(2 * couples):
+                    sums[owners + which, :, lanes] = product[which * rows : (which + 1) * rows]
+
+            @pl.when(part > 0)
+            def _():
+                for which in range(2 * couples):
+                    sums[owners + which, :, lanes] += product[which * rows : (which + 1) * rows]
+
+        @pl.when(part == parts - 1)
+        def _():
+            start_pairs(stage)
+
+            @pl.when(stage >= 1)
+            def _():
+                finish_pairs(stage - 1)
 
     @pl.when(step == chunks)
     def _():
-        exchange(chunks - 2).wait_send()
-        exchange(chunks - 1).wait_send()
+        finish_pairs(pieces - 1)
+        total = paired[me // 2]
+        for away in range(1, pairs):
+            source = (me // 2 + pairs - away) % pairs
+            owner_copy((me // 2 + away) % pairs, source).wait_recv()
+            total = total + landed[source]
+        out_ref[...] = total
+        for away in range(1, pairs):
+            owner_copy((me // 2 + away) % pairs, me // 2).wait_send()
+        for couple in range(pairs):
+            pair_copy(couple).wait_send()
+        exchange(chunks - 2, few).wait_send()
+        exchange(chunks - 1, few).wait_send()
 
 
 def convolve(mix, x_own, snap_first, snap_second, groups):
     snaps, taps, rows, width = snap_first.shape
     members, tokens = mix.shape[0] // 2, x_own.shape[1]
-    pair = (members, rows, width)
+    span = math.lcm(128, 2 * rows)
+    few = 3
+    pieces, parts = width // span, taps // few
+    couples, pairs = span // (2 * rows), groups // 2
+    part = (members, max(pieces, few), rows, span)
+    sums = (rows, members * tokens)
+
+    def second_block(i):
+        at = jnp.clip(i - taps, 0, pieces * parts - 1)
+        piece = (lax.axis_index("mp") // (2 * couples) + at // parts + 1) % pieces
+        return 0, at % parts, 0, piece
+
     return pl.pallas_call(
-        functools.partial(conv_kernel, taps, groups),
-        grid=(2 * taps + 1,),
-        out_shape=jax.ShapeDtypeStruct((width, members * tokens), jnp.float32),
+        functools.partial(conv_kernel, taps, groups, span, few),
+        grid=(taps + pieces * parts + 1,),
+        out_shape=jax.ShapeDtypeStruct(sums, jnp.float32),
         in_specs=[
             pl.BlockSpec(memory_space=pltpu.SMEM),
             pl.BlockSpec((rows, tokens), lambda i: (0, 0)),
             pl.BlockSpec((snaps, 1, rows, width), lambda i: (0, jnp.minimum(i, taps - 1), 0, 0)),
-            pl.BlockSpec(
-                (snaps, 1, rows, width), lambda i: (0, jnp.clip(i - taps, 0, taps - 1), 0, 0)
-            ),
+            pl.BlockSpec((snaps, few, rows, span), second_block),
         ],
-        out_specs=pl.BlockSpec((width, members * tokens), lambda i: (0, 0)),
+        out_specs=pl.BlockSpec(sums, lambda i: (0, 0)),
         scratch_shapes=[
-            pltpu.VMEM((2,) + pair, jnp.float32),
-            pltpu.VMEM((2,) + pair, jnp.float32),
-            pltpu.VMEM((4,) + pair, jnp.float32),
+            pltpu.VMEM((2,) + part, jnp.float32),
+            pltpu.VMEM((2,) + part, jnp.float32),
+            pltpu.VMEM((4,) + part, jnp.float32),
             pltpu.VMEM((groups, rows, tokens), jnp.bfloat16),
             pltpu.VMEM((width, tokens), jnp.bfloat16),
             pltpu.VMEM((members, rows, tokens), jnp.float32),
             pltpu.VMEM((members, rows, tokens), jnp.bfloat16),
+            pltpu.VMEM((groups,) + sums, jnp.float32),
+            pltpu.VMEM((pairs,) + sums, jnp.float32),
+            pltpu.VMEM((pairs,) + sums, jnp.float32),
             pltpu.SemaphoreType.DMA((2,)),
             pltpu.SemaphoreType.DMA((4,)),
             pltpu.SemaphoreType.DMA((groups,)),
             pltpu.SemaphoreType.DMA((groups,)),
+            pltpu.SemaphoreType.DMA((pairs,)),
+            pltpu.SemaphoreType.DMA((pairs,)),
+            pltpu.SemaphoreType.DMA((pairs,)),
+            pltpu.SemaphoreType.DMA((pairs,)),
         ],
         compiler_params=pltpu.CompilerParams(
             collective_id=0,
@@ -294,8 +391,7 @@
     first_slot = lax.axis_index("cand") * owned
     mix = lax.dynamic_slice_in_dim(jnp.concatenate([mixing, other_mix], 0), first_slot, owned, 1)
     members = blend.shape[0]
-    sums = convolve(mix, x_own, snap_first, snap_second, groups)
-    feature = lax.psum_scatter(sums, "mp", scatter_dimension=0, tiled=True)
+    feature = convolve(mix, x_own, snap_first, snap_second, groups)
     tokens = clean.shape[1]
     features = jnp.stack([feature[:, c * tokens : (c + 1) * tokens] for c in range(members)], 0)
     denoised_f = scale_skip[None, None, :] * noisy[None] + scale_out[None, None, :] * features

time: 241 us -> 173 us (0.72)
  waiting for transfers between devices: 103 us -> 0.01 us
  Pallas kernels: 113 us -> 160 us
  between operations: 14.1 us -> 0.66 us
    reduce_scatter x1 -> x0, waiting for transfers between devices: 103 us -> none  [on_device(): feature = lax.psum_scatter(sums, 'mp', scatter_dimension=0, tiled=True)]
    pallas_call x1, Pallas kernels: 104 us -> 150 us  [convolve(): pl.pallas_call(functools.partial(conv_kernel, taps, groups, span, few), g...]
  transfers between devices with their start and end apart: 2 -> 1, of which waited for: 1 -> 0; matrix products, arithmetic and copies ran while one was open for 2% -> 3% of each run, Pallas kernels for 0% -> 0%
where the time goes in v2:
time: 173 us
  Pallas kernels  160 us (92%)
  other arithmetic  8.71 us (5%)
  local copies, waits for them, and re-layouts  2.55 us (1%)
    pallas_call x1, Pallas kernels, convolve(): pl.pallas_call(functools.partial(conv_kernel, taps, groups, span, few), g...  150 us
    pallas_call x1, Pallas kernels, total_over(): pl.pallas_call(functools.partial(total_kernel, groups, images), out_shape...  9.83 us
  transfers between devices with their start and end apart: 1, of which 0 were waited for; matrix products, arithmetic and copies ran while one was open for 3% of the time, Pallas kernels for 0%

profile of v2, /device:TPU:0, one launch (start us, length us, event | category | flops | bytes accessed | tf_op | source)
XLA Modules:
  0.0 172.5 jit_solution(9260565759171126848)
XLA Ops:
  0.6 0.8 select_reduce_fusion
  1.4 0.6 collective-permute-start
  2.0 0.7 add_exponential_fusion
  2.6 0.1 broadcast_in_dim.4
  2.7 0.1 reshape.48
  2.8 0.6 multiply_divide_fusion
  3.4 1.6 convert_element_type.19
  5.0 1.8 %fusion.2 = (f32[192,384]{1,0:T(8,128)}, bf16[192,384]{1,0:T(8,128)(2,1)}) fusion(bf16[192,384]{1,0:T(8,128)(2,1)} %param.8, f32[384]{0:T(512)S(1)} %reshape.48, bf16[192,384]{1,0:T(8,128)(2,1)} %param.7, f32[384]{0:T(512)S(1)} %get-tuple-element.11, f32[384]{0:T(512)S(1)} %get-tuple-element.9), kind=kLoop, calls=%fused_computation.8 | loop fusion | flops 516096 | bytes 741888 | tf_op jit(solution)/shard_map/mul | solution.py:397
  6.8 0.0 collective-permute-done
  6.8 0.6 constant_dynamic-slice_fusion.mix_ref
  7.5 150.2 %blend_convolve.1 = f32[192,768]{1,0:T(8,128)} custom-call(f32[4,8]{1,0:T(4,128)} %constant_dynamic-slice_fusion.mix_ref, bf16[192,384]{1,0:T(8,128)(2,1)} %get-tuple-element.7.x_ref, bf16[8,9,192,1536]{3,2,1,0:T(8,128)(2,1)} %first_ref.1, bf16[8,9,192,1536]{3,2,1,0:T(8,128)(2,1)} %second_ref.1), custom_call_target="tpu_custom_call" | custom-call | tf_op jit(solution)/shard_map/blend_convolve/pallas_call | solution.py:279
  157.7 1.1 slice_bitcast_fusion.1
  158.8 1.9 %fusion.1 = (bf16[2,192,384]{2,1,0:T(8,128)(2,1)}, f32[2]{0:T(128)S(1)}) fusion(f32[1,192,384]{2,1,0:T(8,128)S(1)} %get-tuple-element.5, f32[1,192,384]{2,1,0:T(8,128)S(1)} %get-tuple-element.4, f32[384]{0:T(512)} %get-tuple-element.10, f32[192,384]{1,0:T(8,128)} %get-tuple-element.6, f32[192,384]{1,0:T(8,128)} %convert_element_type.19, f32[384]{0:T(512)} %get-tuple-element.8), kind=kLoop, calls=%fused_computation.3 | loop fusion | flops 1179646 | bytes 1477640 | tf_op jit(solution)/shard_map/convert_element_type | solution.py:404
  160.7 0.7 broadcast_in_dim.5.own_ref
  161.4 9.8 %loss_total.1 = f32[8,128]{1,0:T(8,128)} custom-call(f32[8,128]{1,0:T(8,128)} %broadcast_in_dim.5.own_ref), custom_call_target="tpu_custom_call" | custom-call | tf_op jit(solution)/shard_map/loss_total/pallas_call | solution.py:358
  171.2 1.3 multiply_reduce_fusion.1
  (2 shorter events, 0.0 us)
Async XLA Ops:
  1.4 5.4 %collective-permute-start = (f32[2,16]{1,0:T(2,128)S(1)}, f32[2,16]{1,0:T(2,128)S(1)}, u32[]{:S(2)}, u32[]{:S(2)}) collective-permute-start(f32[2,16]{1,0:T(2,128)S(1)} %select_reduce_fusion), channel_id=1, source_target_pairs={{0,16},{16,0},{1,17},{17,1},{2,18},{18,2},{3,19},{19,3},{4,20},{20... | collective-permute-start | bytes 392 | tf_op jit(solution)/shard_map/ppermute | solution.py:17

commit v3 on v2

--- a/solution.py
+++ b/solution.py
@@ -35,16 +35,18 @@
 
 
 def conv_kernel(
-    taps, groups, span, few, mix_ref, x_ref, first_ref, second_ref, out_ref,
+    taps, groups, span, few, members, mix_ref, x_ref, first_ref, second_ref, out_ref,
     give, mine, got, x_full, x_tap, pre, hidden, sums, paired, landed,
     send_sem, recv_sem, x_send, x_recv, pair_send, pair_recv, owner_send, owner_recv,
 ):
     step = pl.program_id(0)
     snaps, rows, width = first_ref.shape[0], first_ref.shape[2], first_ref.shape[3]
-    members, tokens = pre.shape[0], pre.shape[2]
+    tokens = pre.shape[1]
     tiles = tokens // 128
     pieces, parts = width // span, taps // few
-    chunks = taps + pieces * parts
+    per = taps + pieces * parts
+    chunks = members * per
+    member, local = step // per, step % per
     pairs, couples = groups // 2, span // (2 * rows)
     cand, me = lax.axis_index("cand"), lax.axis_index("mp")
     partner = 1 - cand
@@ -54,8 +56,8 @@
 
     def exchange(chunk, count):
         return pltpu.make_async_remote_copy(
-            src_ref=give.at[chunk % 2, :, pl.ds(0, count)],
-            dst_ref=got.at[chunk % 4, :, pl.ds(0, count)],
+            src_ref=give.at[chunk % 2, pl.ds(0, count)],
+            dst_ref=got.at[chunk % 4, pl.ds(0, count)],
             send_sem=send_sem.at[chunk % 2],
             recv_sem=recv_sem.at[chunk % 4],
             device_id={"cand": partner},
@@ -75,39 +77,41 @@
     def piece_of(stage):
         return (my_piece + stage + 1) % pieces
 
-    def pair_copy(couple):
+    def pair_copy(which, couple):
         return pltpu.make_async_remote_copy(
-            src_ref=sums.at[2 * couple + 1 - side],
-            dst_ref=paired.at[couple],
-            send_sem=pair_send.at[couple],
-            recv_sem=pair_recv.at[couple],
+            src_ref=sums.at[which * groups + 2 * couple + 1 - side],
+            dst_ref=paired.at[which * pairs + couple],
+            send_sem=pair_send.at[which * pairs + couple],
+            recv_sem=pair_recv.at[which * pairs + couple],
             device_id={"mp": me + 1 - 2 * side},
             device_id_type=MESH,
         )
 
-    def owner_copy(couple, slot):
+    def owner_copy(which, couple, slot):
         return pltpu.make_async_remote_copy(
-            src_ref=paired.at[couple],
-            dst_ref=landed.at[slot],
-            send_sem=owner_send.at[couple],
-            recv_sem=owner_recv.at[slot],
+            src_ref=paired.at[which * pairs + couple],
+            dst_ref=landed.at[which * pairs + slot],
+            send_sem=owner_send.at[which * pairs + couple],
+            recv_sem=owner_recv.at[which * pairs + slot],
             device_id={"mp": 2 * couple + side},
             device_id_type=MESH,
         )
 
     def start_pairs(stage):
-        for which in range(couples):
-            pair_copy(piece_of(stage) * couples + which).start()
+        for index in range(couples):
+            pair_copy(stage // pieces, piece_of(stage % pieces) * couples + index).start()
 
     def finish_pairs(stage):
-        for which in range(couples):
-            couple = piece_of(stage) * couples + which
-            pair_copy(couple).wait_recv()
-            paired[couple] = paired[couple] + sums[2 * couple + side]
+        which = stage // pieces
+        for index in range(couples):
+            couple = piece_of(stage % pieces) * couples + index
+            pair_copy(which, couple).wait_recv()
+            at = which * pairs + couple
+            paired[at] = paired[at] + sums[which * groups + 2 * couple + side]
 
             @pl.when(couple != me // 2)
             def _():
-                owner_copy(couple, me // 2).start()
+                owner_copy(which, couple, me // 2).start()
 
     @pl.when(step == 0)
     def _():
@@ -121,10 +125,9 @@
         for away in range(1, groups):
             x_copy(away, me).start()
         x_full[me] = x_ref[...]
-        pre[...] = jnp.zeros_like(pre)
 
     def blend(source, count, columns, place):
-        coeff = [[mix_ref[c, s] for s in range(snaps)] for c in range(2 * members)]
+        coeff = [[mix_ref[c + member, s] for s in range(snaps)] for c in (0, members)]
         slot = step % 2
 
         def body(which, carry):
@@ -132,34 +135,35 @@
             for tap in range(count):
                 for tile in range(columns // 128):
                     lanes = pl.ds(tile * 128, 128)
-                    totals = [None] * (2 * members)
+                    totals = [None, None]
                     for s in range(snaps):
                         value = source[s, tap, at, lanes].astype(jnp.float32)
-                        for c in range(2 * members):
+                        for c in range(2):
                             term = coeff[c][s] * value
                             totals[c] = term if s == 0 else totals[c] + term
                     piece, first = place(tap, tile)
-                    for c in range(members):
-                        mine[slot, c, piece, at, pl.ds(first, 128)] = totals[c]
-                        give[slot, c, piece, at, pl.ds(first, 128)] = totals[members + c]
+                    mine[slot, piece, at, pl.ds(first, 128)] = totals[0]
+                    give[slot, piece, at, pl.ds(first, 128)] = totals[1]
             return carry
 
         lax.fori_loop(0, rows // block, body, 0)
 
-    @pl.when((step >= 2) & (step < taps + 2))
+    earlier = (step + per - 2) % per
+
+    @pl.when((step >= 2) & (step < chunks) & (earlier < taps))
     def _():
         exchange(step - 2, pieces).wait_send()
 
-    @pl.when((step >= taps + 2) & (step < chunks))
+    @pl.when((step >= 2) & (step < chunks) & (earlier >= taps))
     def _():
         exchange(step - 2, few).wait_send()
 
-    @pl.when(step < taps)
+    @pl.when((step < chunks) & (local < taps))
     def _():
         blend(first_ref, 1, width, lambda tap, tile: (tile * 128 // span, tile * 128 % span))
         exchange(step, pieces).start()
 
-    @pl.when((step >= taps) & (step < chunks))
+    @pl.when((step < chunks) & (local >= taps))
     def _():
         blend(second_ref, few, span, lambda tap, tile: (tap, tile * 128))
         exchange(step, few).start()
@@ -172,42 +176,54 @@
             copy.wait_recv()
 
     done = step - 1
-
-    def weight_of(c, piece):
-        return (mine[done % 2, c, piece] + got[done % 4, c, piece]).astype(jnp.bfloat16)
+    past = (step + per - 1) % per
+
+    def weight_of(piece):
+        return (mine[done % 2, piece] + got[done % 4, piece]).astype(jnp.bfloat16)
 
     @pl.when((step >= 1) & (done < taps))
     def _():
-        shift = tap_matrix(done)
+        shift = tap_matrix(past)
         for group in range(groups):
             for tile in range(tiles):
                 lanes = pl.ds(tile * 128, 128)
-                x_tap[pl.ds(group * rows, rows), lanes] = jnp.dot(
+                x_tap[past, pl.ds(group * rows, rows), lanes] = jnp.dot(
                     x_full[group, :, lanes], shift, preferred_element_type=jnp.float32
                 ).astype(jnp.bfloat16)
+
+    @pl.when((step >= 1) & (past < taps))
+    def _():
         exchange(done, pieces).wait_recv()
-        for c in range(members):
-            weight = jnp.concatenate([weight_of(c, piece) for piece in range(pieces)], axis=1)
-            pre[c] += jnp.dot(weight, x_tap[...], preferred_element_type=jnp.float32)
-
-    @pl.when(done == taps - 1)
+        weight = jnp.concatenate([weight_of(piece) for piece in range(pieces)], axis=1)
+        product = jnp.dot(weight, x_tap[past], preferred_element_type=jnp.float32)
+
+        @pl.when(past == 0)
+        def _():
+            pre[...] = product
+
+        @pl.when(past > 0)
+        def _():
+            pre[...] += product
+
+    @pl.when((step >= 1) & (past == taps - 1))
     def _():
         value = pre[...]
         hidden[...] = (value * jax.nn.sigmoid(value)).astype(jnp.bfloat16)
 
-    @pl.when((step >= 1) & (done >= taps))
-    def _():
-        at = done - taps
-        stage, part = at // parts, at % parts
-        owners = piece_of(stage) * 2 * couples
-        shifts = [tap_matrix(part * few + tap) for tap in range(few)]
+    @pl.when((step >= 1) & (past >= taps))
+    def _():
+        stage, part = (past - taps) // parts, (past - taps) % parts
+        which = done // per
+        owners = which * groups + piece_of(stage) * 2 * couples
         exchange(done, few).wait_recv()
-        for c in range(members):
-            moved = [
+        moved = []
+        for tap in range(few):
+            shift = tap_matrix(part * few + tap)
+            moved.append(
                 jnp.concatenate(
                     [
                         jnp.dot(
-                            hidden[c, :, pl.ds(tile * 128, 128)],
+                            hidden[:, pl.ds(tile * 128, 128)],
                             shift,
                             preferred_element_type=jnp.float32,
                         ).astype(jnp.bfloat16)
@@ -215,48 +231,48 @@
                     ],
                     axis=1,
                 )
-                for shift in shifts
-            ]
-            weight = jnp.concatenate([weight_of(c, tap) for tap in range(few)], axis=0)
-            product = lax.dot_general(
-                weight,
-                jnp.concatenate(moved, axis=0),
-                (((0,), (0,)), ((), ())),
-                preferred_element_type=jnp.float32,
             )
-            lanes = pl.ds(c * tokens, tokens)
-
-            @pl.when(part == 0)
-            def _():
-                for which in range(2 * couples):
-                    sums[owners + which, :, lanes] = product[which * rows : (which + 1) * rows]
-
-            @pl.when(part > 0)
-            def _():
-                for which in range(2 * couples):
-                    sums[owners + which, :, lanes] += product[which * rows : (which + 1) * rows]
+        product = lax.dot_general(
+            jnp.concatenate([weight_of(tap) for tap in range(few)], axis=0),
+            jnp.concatenate(moved, axis=0),
+            (((0,), (0,)), ((), ())),
+            preferred_element_type=jnp.float32,
+        )
+
+        @pl.when(part == 0)
+        def _():
+            for index in range(2 * couples):
+                sums[owners + index] = product[index * rows : (index + 1) * rows]
+
+        @pl.when(part > 0)
+        def _():
+            for index in range(2 * couples):
+                sums[owners + index] += product[index * rows : (index + 1) * rows]
 
         @pl.when(part == parts - 1)
         def _():
-            start_pairs(stage)
-
-            @pl.when(stage >= 1)
+            overall = which * pieces + stage
+            start_pairs(overall)
+
+            @pl.when(overall >= 1)
             def _():
-                finish_pairs(stage - 1)
+                finish_pairs(overall - 1)
 
     @pl.when(step == chunks)
     def _():
-        finish_pairs(pieces - 1)
-        total = paired[me // 2]
-        for away in range(1, pairs):
-            source = (me // 2 + pairs - away) % pairs
-            owner_copy((me // 2 + away) % pairs, source).wait_recv()
-            total = total + landed[source]
-        out_ref[...] = total
-        for away in range(1, pairs):
-            owner_copy((me // 2 + away) % pairs, me // 2).wait_send()
-        for couple in range(pairs):
-            pair_copy(couple).wait_send()
+        finish_pairs(members * pieces - 1)
+        for which in range(members):
+            total = paired[which * pairs + me // 2]
+            for away in range(1, pairs):
+                source = (me // 2 + pairs - away) % pairs
+                owner_copy(which, (me // 2 + away) % pairs, source).wait_recv()
+                total = total + landed[which * pairs + source]
+            out_ref[which] = total
+        for which in range(members):
+            for away in range(1, pairs):
+                owner_copy(which, (me // 2 + away) % pairs, me // 2).wait_send()
+            for couple in range(pairs):
+                pair_copy(which, couple).wait_send()
         exchange(chunks - 2, few).wait_send()
         exchange(chunks - 1, few).wait_send()
 
@@ -268,44 +284,48 @@
     few = 3
     pieces, parts = width // span, taps // few
     couples, pairs = span // (2 * rows), groups // 2
-    part = (members, max(pieces, few), rows, span)
-    sums = (rows, members * tokens)
+    part = (max(pieces, few), rows, span)
+    per = taps + pieces * parts
+    sums = (rows, tokens)
+
+    def local(i):
+        return jnp.minimum(i, members * per - 1) % per
 
     def second_block(i):
-        at = jnp.clip(i - taps, 0, pieces * parts - 1)
+        at = jnp.maximum(local(i) - taps, 0)
         piece = (lax.axis_index("mp") // (2 * couples) + at // parts + 1) % pieces
         return 0, at % parts, 0, piece
 
     return pl.pallas_call(
-        functools.partial(conv_kernel, taps, groups, span, few),
-        grid=(taps + pieces * parts + 1,),
-        out_shape=jax.ShapeDtypeStruct(sums, jnp.float32),
+        functools.partial(conv_kernel, taps, groups, span, few, members),
+        grid=(members * per + 1,),
+        out_shape=jax.ShapeDtypeStruct((members,) + sums, jnp.float32),
         in_specs=[
             pl.BlockSpec(memory_space=pltpu.SMEM),
             pl.BlockSpec((rows, tokens), lambda i: (0, 0)),
-            pl.BlockSpec((snaps, 1, rows, width), lambda i: (0, jnp.minimum(i, taps - 1), 0, 0)),
+            pl.BlockSpec((snaps, 1, rows, width), lambda i: (0, jnp.minimum(local(i), taps - 1), 0, 0)),
             pl.BlockSpec((snaps, few, rows, span), second_block),
         ],
-        out_specs=pl.BlockSpec(sums, lambda i: (0, 0)),
+        out_specs=pl.BlockSpec((members,) + sums, lambda i: (0, 0, 0)),
         scratch_shapes=[
             pltpu.VMEM((2,) + part, jnp.float32),
             pltpu.VMEM((2,) + part, jnp.float32),
             pltpu.VMEM((4,) + part, jnp.float32),
             pltpu.VMEM((groups, rows, tokens), jnp.bfloat16),
-            pltpu.VMEM((width, tokens), jnp.bfloat16),
-            pltpu.VMEM((members, rows, tokens), jnp.float32),
-            pltpu.VMEM((members, rows, tokens), jnp.bfloat16),
-            pltpu.VMEM((groups,) + sums, jnp.float32),
-            pltpu.VMEM((pairs,) + sums, jnp.float32),
-            pltpu.VMEM((pairs,) + sums, jnp.float32),
+            pltpu.VMEM((taps, width, tokens), jnp.bfloat16),
+            pltpu.VMEM(sums, jnp.float32),
+            pltpu.VMEM(sums, jnp.bfloat16),
+            pltpu.VMEM((members * groups,) + sums, jnp.float32),
+            pltpu.VMEM((members * pairs,) + sums, jnp.float32),
+            pltpu.VMEM((members * pairs,) + sums, jnp.float32),
             pltpu.SemaphoreType.DMA((2,)),
             pltpu.SemaphoreType.DMA((4,)),
             pltpu.SemaphoreType.DMA((groups,)),
             pltpu.SemaphoreType.DMA((groups,)),
-            pltpu.SemaphoreType.DMA((pairs,)),
-            pltpu.SemaphoreType.DMA((pairs,)),
-            pltpu.SemaphoreType.DMA((pairs,)),
-            pltpu.SemaphoreType.DMA((pairs,)),
+            pltpu.SemaphoreType.DMA((members * pairs,)),
+            pltpu.SemaphoreType.DMA((members * pairs,)),
+            pltpu.SemaphoreType.DMA((members * pairs,)),
+            pltpu.SemaphoreType.DMA((members * pairs,)),
         ],
         compiler_params=pltpu.CompilerParams(
             collective_id=0,
@@ -391,9 +411,7 @@
     first_slot = lax.axis_index("cand") * owned
     mix = lax.dynamic_slice_in_dim(jnp.concatenate([mixing, other_mix], 0), first_slot, owned, 1)
     members = blend.shape[0]
-    feature = convolve(mix, x_own, snap_first, snap_second, groups)
-    tokens = clean.shape[1]
-    features = jnp.stack([feature[:, c * tokens : (c + 1) * tokens] for c in range(members)], 0)
+    features = convolve(mix, x_own, snap_first, snap_second, groups)
     denoised_f = scale_skip[None, None, :] * noisy[None] + scale_out[None, None, :] * features
     partial_value = jnp.sum(
         weighting[None, None, :] * (denoised_f - clean_f[None]) ** 2, axis=(1, 2)

time: 173 us -> 176 us (1.017)
  Pallas kernels: 160 us -> 164 us
    pallas_call x1, Pallas kernels: 150 us -> 155 us  [convolve(): pl.pallas_call(functools.partial(conv_kernel, taps, groups, span, few, me...]
where the time goes in v3:
time: 176 us
  Pallas kernels  164 us (93%)
  other arithmetic  8.89 us (5%)
    pallas_call x1, Pallas kernels, convolve(): pl.pallas_call(functools.partial(conv_kernel, taps, groups, span, few, me...  155 us
    pallas_call x1, Pallas kernels, total_over(): pl.pallas_call(functools.partial(total_kernel, groups, images), out_shape...  8.88 us
  transfers between devices with their start and end apart: 1, of which 0 were waited for; matrix products, arithmetic and copies ran while one was open for 3% of the time, Pallas kernels for 0%

profile of v3, /device:TPU:0, one launch (start us, length us, event | category | flops | bytes accessed | tf_op | source)
XLA Modules:
  0.0 175.8 jit_solution(181545794750409272)
XLA Ops:
  0.6 0.8 select_reduce_fusion
  1.4 0.6 collective-permute-start
  2.0 0.7 add_exponential_fusion
  2.6 0.1 broadcast_in_dim.4
  2.7 0.1 reshape.48
  2.8 0.6 multiply_divide_fusion
  3.4 1.6 convert_element_type.19
  5.0 1.8 %fusion.1 = (f32[192,384]{1,0:T(8,128)}, bf16[192,384]{1,0:T(8,128)(2,1)}) fusion(bf16[192,384]{1,0:T(8,128)(2,1)} %param.8, f32[384]{0:T(512)S(1)} %reshape.48, bf16[192,384]{1,0:T(8,128)(2,1)} %param.7, f32[384]{0:T(512)S(1)} %get-tuple-element.9, f32[384]{0:T(512)S(1)} %get-tuple-element.7), kind=kLoop, calls=%fused_computation.5 | loop fusion | flops 516096 | bytes 741888 | tf_op jit(solution)/shard_map/mul | solution.py:415
  6.8 0.0 collective-permute-done
  6.8 0.6 constant_dynamic-slice_fusion.mix_ref
  7.5 155.4 %blend_convolve.1 = f32[2,192,384]{2,1,0:T(8,128)} custom-call(f32[4,8]{1,0:T(4,128)} %constant_dynamic-slice_fusion.mix_ref, bf16[192,384]{1,0:T(8,128)(2,1)} %get-tuple-element.5.x_ref, bf16[8,9,192,1536]{3,2,1,0:T(8,128)(2,1)} %first_ref.1, bf16[8,9,192,1536]{3,2,1,0:T(8,128)(2,1)} %second_ref.1), custom_call_target="tpu_custom_call" | custom-call | tf_op jit(solution)/shard_map/blend_convolve/pallas_call | solution.py:299
  162.8 2.1 %fusion = (bf16[2,192,384]{2,1,0:T(8,128)(2,1)}, f32[2]{0:T(128)S(1)}) fusion(f32[2,192,384]{2,1,0:T(8,128)} %blend_convolve.1, f32[384]{0:T(512)} %get-tuple-element.8, f32[192,384]{1,0:T(8,128)} %get-tuple-element.4, f32[192,384]{1,0:T(8,128)} %convert_element_type.19, f32[384]{0:T(512)} %get-tuple-element.6), kind=kLoop, calls=%fused_computation.2 | loop fusion | flops 1032190 | bytes 1477640 | tf_op jit(solution)/shard_map/convert_element_type | solution.py:422
  165.0 0.7 broadcast_in_dim.5.own_ref
  165.6 8.9 %loss_total.1 = f32[8,128]{1,0:T(8,128)} custom-call(f32[8,128]{1,0:T(8,128)} %broadcast_in_dim.5.own_ref), custom_call_target="tpu_custom_call" | custom-call | tf_op jit(solution)/shard_map/loss_total/pallas_call | solution.py:378
  174.5 1.3 multiply_reduce_fusion.1
  (2 shorter events, 0.0 us)
Async XLA Ops:
  1.4 5.4 %collective-permute-start = (f32[2,16]{1,0:T(2,128)S(1)}, f32[2,16]{1,0:T(2,128)S(1)}, u32[]{:S(2)}, u32[]{:S(2)}) collective-permute-start(f32[2,16]{1,0:T(2,128)S(1)} %select_reduce_fusion), channel_id=1, source_target_pairs={{0,16},{16,0},{1,17},{17,1},{2,18},{18,2},{3,19},{19,3},{4,20},{20... | collective-permute-start | bytes 392 | tf_op jit(solution)/shard_map/ppermute | solution.py:17

commit v4 on v2

--- a/solution.py
+++ b/solution.py
@@ -36,7 +36,7 @@
 
 def conv_kernel(
     taps, groups, span, few, mix_ref, x_ref, first_ref, second_ref, out_ref,
-    give, mine, got, x_full, x_tap, pre, hidden, sums, paired, landed,
+    give, mine, got, x_full, x_tap, pre, hidden, sums, paired, leaving, landed,
     send_sem, recv_sem, x_send, x_recv, pair_send, pair_recv, owner_send, owner_recv,
 ):
     step = pl.program_id(0)
@@ -87,7 +87,7 @@
 
     def owner_copy(couple, slot):
         return pltpu.make_async_remote_copy(
-            src_ref=paired.at[couple],
+            src_ref=leaving.at[couple],
             dst_ref=landed.at[slot],
             send_sem=owner_send.at[couple],
             recv_sem=owner_recv.at[slot],
@@ -103,7 +103,9 @@
         for which in range(couples):
             couple = piece_of(stage) * couples + which
             pair_copy(couple).wait_recv()
-            paired[couple] = paired[couple] + sums[2 * couple + side]
+            total = paired[couple] + sums[2 * couple + side]
+            paired[couple] = total
+            leaving[couple] = total.astype(jnp.bfloat16)
 
             @pl.when(couple != me // 2)
             def _():
@@ -251,7 +253,7 @@
         for away in range(1, pairs):
             source = (me // 2 + pairs - away) % pairs
             owner_copy((me // 2 + away) % pairs, source).wait_recv()
-            total = total + landed[source]
+            total = total + landed[source].astype(jnp.float32)
         out_ref[...] = total
         for away in range(1, pairs):
             owner_copy((me // 2 + away) % pairs, me // 2).wait_send()
@@ -297,7 +299,8 @@
             pltpu.VMEM((members, rows, tokens), jnp.bfloat16),
             pltpu.VMEM((groups,) + sums, jnp.float32),
             pltpu.VMEM((pairs,) + sums, jnp.float32),
-            pltpu.VMEM((pairs,) + sums, jnp.float32),
+            pltpu.VMEM((pairs,) + sums, jnp.bfloat16),
+            pltpu.VMEM((pairs,) + sums, jnp.bfloat16),
             pltpu.SemaphoreType.DMA((2,)),
             pltpu.SemaphoreType.DMA((4,)),
             pltpu.SemaphoreType.DMA((groups,)),

time: 173 us -> 158 us (0.913)
  Pallas kernels: 160 us -> 145 us
    pallas_call x1, Pallas kernels: 150 us -> 131 us  [convolve(): pl.pallas_call(functools.partial(conv_kernel, taps, groups, span, few), g...]
    pallas_call x1, Pallas kernels: 9.83 us -> 13.7 us  [total_over(): pl.pallas_call(functools.partial(total_kernel, groups, images), out_shape...]
where the time goes in v4:
time: 158 us
  Pallas kernels  145 us (92%)
  other arithmetic  8.71 us (6%)
  local copies, waits for them, and re-layouts  2.55 us (2%)
    pallas_call x1, Pallas kernels, convolve(): pl.pallas_call(functools.partial(conv_kernel, taps, groups, span, few), g...  131 us
    pallas_call x1, Pallas kernels, total_over(): pl.pallas_call(functools.partial(total_kernel, groups, images), out_shape...  13.7 us
  transfers between devices with their start and end apart: 1, of which 0 were waited for; matrix products, arithmetic and copies ran while one was open for 3% of the time, Pallas kernels for 0%

profile of v4, /device:TPU:0, one launch (start us, length us, event | category | flops | bytes accessed | tf_op | source)
XLA Modules:
  0.0 157.5 jit_solution(11533953107814888023)
XLA Ops:
  0.6 0.8 select_reduce_fusion
  1.4 0.6 collective-permute-start
  2.0 0.7 add_exponential_fusion
  2.6 0.1 broadcast_in_dim.4
  2.7 0.1 reshape.48
  2.8 0.6 multiply_divide_fusion
  3.4 1.6 %convert_element_type.19 = f32[192,384]{1,0:T(8,128)} convert(bf16[192,384]{1,0:T(8,128)(2,1)} %param.7) | non-fusion elementwise | flops 73728 | bytes 442368 | tf_op jit(solution)/shard_map/convert_element_type | solution.py:383
  5.0 1.8 %fusion.2 = (f32[192,384]{1,0:T(8,128)}, bf16[192,384]{1,0:T(8,128)(2,1)}) fusion(bf16[192,384]{1,0:T(8,128)(2,1)} %param.8, f32[384]{0:T(512)S(1)} %reshape.48, bf16[192,384]{1,0:T(8,128)(2,1)} %param.7, f32[384]{0:T(512)S(1)} %get-tuple-element.11, f32[384]{0:T(512)S(1)} %get-tuple-element.9), kind=kLoop, calls=%fused_computation.8 | loop fusion | flops 516096 | bytes 741888 | tf_op jit(solution)/shard_map/mul | solution.py:400
  6.8 0.0 collective-permute-done
  6.8 0.6 constant_dynamic-slice_fusion.mix_ref
  7.5 131.4 %blend_convolve.1 = f32[192,768]{1,0:T(8,128)} custom-call(f32[4,8]{1,0:T(4,128)} %constant_dynamic-slice_fusion.mix_ref, bf16[192,384]{1,0:T(8,128)(2,1)} %get-tuple-element.7.x_ref, bf16[8,9,192,1536]{3,2,1,0:T(8,128)(2,1)} %first_ref.1, bf16[8,9,192,1536]{3,2,1,0:T(8,128)(2,1)} %second_ref.1), custom_call_target="tpu_custom_call" | custom-call | tf_op jit(solution)/shard_map/blend_convolve/pallas_call | solution.py:281
  138.8 1.1 slice_bitcast_fusion.1
  139.9 1.9 %fusion.1 = (bf16[2,192,384]{2,1,0:T(8,128)(2,1)}, f32[2]{0:T(128)S(1)}) fusion(f32[1,192,384]{2,1,0:T(8,128)S(1)} %get-tuple-element.5, f32[1,192,384]{2,1,0:T(8,128)S(1)} %get-tuple-element.4, f32[384]{0:T(512)} %get-tuple-element.10, f32[192,384]{1,0:T(8,128)} %get-tuple-element.6, f32[192,384]{1,0:T(8,128)} %convert_element_type.19, f32[384]{0:T(512)} %get-tuple-element.8), kind=kLoop, calls=%fused_computation.3 | loop fusion | flops 1179646 | bytes 1477640 | tf_op jit(solution)/shard_map/convert_element_type | solution.py:407
  141.9 0.7 broadcast_in_dim.5.own_ref
  142.5 13.7 %loss_total.1 = f32[8,128]{1,0:T(8,128)} custom-call(f32[8,128]{1,0:T(8,128)} %broadcast_in_dim.5.own_ref), custom_call_target="tpu_custom_call" | custom-call | tf_op jit(solution)/shard_map/loss_total/pallas_call | solution.py:361
  156.2 1.3 multiply_reduce_fusion.1
  (2 shorter events, 0.0 us)
Async XLA Ops:
  1.4 5.4 %collective-permute-start = (f32[2,16]{1,0:T(2,128)S(1)}, f32[2,16]{1,0:T(2,128)S(1)}, u32[]{:S(2)}, u32[]{:S(2)}) collective-permute-start(f32[2,16]{1,0:T(2,128)S(1)} %select_reduce_fusion), channel_id=1, source_target_pairs={{0,16},{16,0},{1,17},{17,1},{2,18},{18,2},{3,19},{19,3},{4,20},{20... | collective-permute-start | bytes 392 | tf_op jit(solution)/shard_map/ppermute | solution.py:17
